TPU v7x, 256 devices: a whole 4x4x8 slice. The times are simulated.
256 devices in a mesh: seq: 16 (over y, x), pack: 16 (over z, core).
Axes of the slice: x: 4, y: 4, z: 8, core: 2. Of those that a mesh axis runs over, the one named last changes fastest.
Arguments:
- patches: bfloat16 [16, 3072, 1408], P('pack', 'seq'), may hold values from -80 to 80
- patch_mask: int32 [16, 3072], P('pack', 'seq'), may hold values 0 or 1
- mask_embed: bfloat16 [1408], replicated, may hold values from -6 to 6
- norm_gain: bfloat16 [1408], replicated, may hold values from 0.5 to 1.5
- qkv_weight: bfloat16 [1408, 4224], P(None, 'seq'), may hold values from -1 to 1
- segment_ids: int32 [16, 3072], P('pack', 'seq'), may hold values from 0 to 7, as said below
- patch_rows: int32 [16, 3072], P('pack', 'seq'), may hold values from 0 to 23, as said below
- patch_column: int32 [16, 3072], P('pack', 'seq'), may hold values from 0 to 31, as said below
- out_weight: bfloat16 [1408, 1408], replicated, may hold values from -0.625 to 0.625
- merge_gain: bfloat16 [1408], replicated, may hold values from 0.5 to 1.5
- merge_weight: bfloat16 [5632, 3584], P(None, 'seq'), may hold values from -0.078125 to 0.078125
- merge_bias: bfloat16 [3584], P('seq'), may hold values from -3 to 3
- image_owner: int32 [16, 8], P('pack'), may hold values from 0 to 15, as said below
Outputs:
- routed: bfloat16 [16, 16, 192, 3584], P('pack', None, None, 'seq')
Inputs may be any that keep to these rules, and one draw needn't show every extreme that they name: `segment_ids`: in each pack the tokens come in aligned groups of four of one image (the four patches of one 2 x 2 window, in merge order); image numbers never fall along a pack; each of the 8 images has 1 to 192 groups and one has exactly 192. `patch_rows`: each image is some number w of windows wide, 1 <= w <= 16; the image with exactly 192 groups has w = 16; group g of an image covers rows 2 (g // w) and 2 (g // w) + 1 and columns 2 (g % w) and 2 (g % w) + 1, in the order (top left, top right, bottom left, bottom right). `patch_column`: as for patch_rows. `image_owner`: in each pack the owners of its 8 images are distinct owner indices, so at most 192 merged tokens go from one pack to one owner; one owner gets a pack's largest image, of exactly 192 merged tokens, from every pack.
All inputs are finite; a program needn't handle non-finite values. No bound on the sum of `patch_mask` on one device may be relied on, other than what follows from the above.
Results may differ from a plain program's by a relative error of at most 0.0061.
Values may be sent and summed in bfloat16 or wider, within the bound.
A program may use at most 64 MiB of HBM per device.

v0:
```python
import jax
import jax.numpy as jnp
from jax import lax
from jax.sharding import PartitionSpec as P

D = 1408
HEADS = 16
HD = 88


EPSILON = 1e-06


def layer_norm(values, gain_vector):
    center = values - jnp.mean(values, axis=-1, keepdims=True)
    spread = jnp.mean(center * center, axis=-1, keepdims=True)
    return center * lax.rsqrt(spread + EPSILON) * gain_vector.astype(jnp.float32)


def rotate(vectors, row_index, column_index):
    total_rows, heads_here, head_width = vectors.shape
    quarter = head_width // 4
    frequency = 10000.0 ** (-jnp.arange(quarter, dtype=jnp.float32) / quarter)
    row_angle = row_index.astype(jnp.float32)[:, None] * frequency[None, :]
    column_angle = column_index.astype(jnp.float32)[:, None] * frequency[None, :]
    angles = jnp.stack([row_angle, column_angle], axis=1)[:, None, :, None, :]
    split_up = vectors.reshape(total_rows, heads_here, 2, 2, quarter)
    partner = jnp.stack([-split_up[:, :, :, 1], split_up[:, :, :, 0]], axis=3)
    turned = split_up * jnp.cos(angles) + partner * jnp.sin(angles)
    return turned.reshape(total_rows, heads_here, head_width)


def qkv_block(projected, row_index, column_index):
    turned_queries = rotate(projected[:, :, 0], row_index, column_index)
    turned_keys = rotate(projected[:, :, 1], row_index, column_index)
    return jnp.concatenate([turned_queries, turned_keys, projected[:, :, 2]], axis=-1).astype(
        jnp.bfloat16
    )


def attention(block, segments):
    total_rows, heads_here, triple = block.shape
    head_width = triple // 3
    step_rows = min(512, total_rows)
    query_part = block[:, :, :head_width].reshape(
        total_rows // step_rows, step_rows, heads_here, head_width
    )
    key_part = block[:, :, head_width : 2 * head_width]
    value_part = block[:, :, 2 * head_width :]
    query_segments = segments.reshape(total_rows // step_rows, step_rows)
    scale = head_width ** (-0.5)

    def one_block(inputs_pair):
        queries_here, segments_here = inputs_pair
        scores = (
            jnp.einsum("qhd,khd->hqk", queries_here, key_part, preferred_element_type=jnp.float32)
            * scale
        )
        same_image = (segments_here[:, None] == segments[None, :])[None]
        scores = jnp.where(same_image, scores, -jnp.inf)
        highest = jnp.max(scores, axis=-1, keepdims=True)
        weights = jnp.exp(scores - highest)
        probs = (weights / jnp.sum(weights, axis=-1, keepdims=True)).astype(jnp.bfloat16)
        result = jnp.einsum("hqk,khd->qhd", probs, value_part, preferred_element_type=jnp.float32)
        return result.astype(jnp.bfloat16)

    return lax.map(one_block, (query_part, query_segments)).reshape(
        total_rows, heads_here, head_width
    )


def route(projected, segments, owners_here, packs, most):
    merged_segments = segments[::4]
    images = owners_here.shape[0]
    image_ids = jnp.arange(images, dtype=jnp.int32)
    member = (merged_segments[None, :] == image_ids[:, None]).astype(jnp.int32)
    lengths = jnp.sum(member, axis=1, dtype=jnp.int32)
    starts = jnp.cumsum(lengths, dtype=jnp.int32) - lengths
    owner_ids = jnp.arange(packs, dtype=jnp.int32)
    owned = owners_here[None, :] == owner_ids[:, None]
    first_row = jnp.sum(jnp.where(owned, starts[None, :], 0), axis=1, dtype=jnp.int32)
    owned_length = jnp.sum(jnp.where(owned, lengths[None, :], 0), axis=1, dtype=jnp.int32)
    slots = jnp.arange(most, dtype=jnp.int32)
    source_rows = jnp.clip(first_row[:, None] + slots[None, :], 0, projected.shape[0] - 1)
    picked = jnp.take(projected, source_rows.reshape(-1), axis=0).reshape(
        packs, most, projected.shape[1]
    )
    filled = slots[None, :] < owned_length[:, None]
    return jnp.where(filled[:, :, None], picked, jnp.zeros_like(picked))


def local(
    patches,
    patch_mask,
    mask_embed,
    norm_gain,
    qkv_weight,
    segment_ids,
    patch_rows,
    patch_column,
    out_weight,
    merge_gain,
    merge_weight,
    merge_bias,
    image_owner,
):
    local_rows = patches.shape[1]
    shards = lax.axis_size("seq")
    packs = lax.axis_size("pack")
    heads_here = HEADS // shards
    inputs = jnp.where(patch_mask[0][:, None] == 1, mask_embed[None, :], patches[0])
    normed = layer_norm(inputs.astype(jnp.float32), norm_gain).astype(jnp.bfloat16)
    labels = lax.all_gather(
        jnp.stack([segment_ids[0], patch_rows[0], patch_column[0]]), "seq", axis=1, tiled=True
    )
    projected = jnp.dot(
        normed,
        lax.all_gather(qkv_weight, "seq", axis=1, tiled=True),
        preferred_element_type=jnp.float32,
    )
    block = qkv_block(projected.reshape(local_rows, HEADS, 3, HD), patch_rows[0], patch_column[0])
    block = block.reshape(local_rows, shards, heads_here, 3 * HD)
    result = attention(
        lax.all_to_all(block, "seq", split_axis=1, concat_axis=0, tiled=True)[:, 0], labels[0]
    )
    mixed_heads = lax.all_to_all(result[:, None], "seq", split_axis=0, concat_axis=1, tiled=True)
    attended = mixed_heads.reshape(local_rows, D)
    residual = inputs.astype(jnp.float32) + jnp.dot(
        attended, out_weight, preferred_element_type=jnp.float32
    )
    merged = layer_norm(residual, merge_gain).astype(jnp.bfloat16).reshape(local_rows // 4, 4 * D)
    projected_all = (
        jnp.dot(
            lax.all_gather(merged, "seq", axis=0, tiled=True),
            merge_weight,
            preferred_element_type=jnp.float32,
        )
        + merge_bias.astype(jnp.float32)
    ).astype(jnp.bfloat16)
    images = image_owner.shape[1]
    most = 2 * projected_all.shape[0] // images
    outgoing = route(projected_all, labels[0], image_owner[0], packs, most)
    delivered = lax.all_to_all(outgoing, "pack", split_axis=0, concat_axis=0, tiled=True)
    return delivered[None]


def solution(mesh):
    placed = (
        P("pack", "seq", None),
        P("pack", "seq"),
        P(),
        P(),
        P(None, "seq"),
        P("pack", "seq"),
        P("pack", "seq"),
        P("pack", "seq"),
        P(),
        P(),
        P(None, "seq"),
        P("seq"),
        P("pack", None),
    )
    return jax.shard_map(
        local, mesh=mesh, in_specs=placed, out_specs=P("pack", None, None, "seq"), check_vma=False
    )
```

profile of v0, /device:TPU:1, one launch (start us, length us, event | category | flops | bytes accessed | tf_op | source)
XLA Modules:
  0.0 434.7 jit_solution(16548475048342397827)
XLA Ops:
  10.4 94.6 %all-gather.4.cloned.1.call-done = bf16[1408,4224]{0,1:T(8,128)(2,1)} async-done(((bf16[1408,264]{0,1:T(8,128)(2,1)}), bf16[1408,4224]{0,1:T(8,128)(2,1)}) %all-gather.4.cloned.1.call-update) | async-done | bytes 11894800 | tf_op jit(solution)/shard_map/all_gather | solution.py:118
  105.0 6.9 %fusion.18 = f32[192,16,3,88]{0,3,2,1:T(8,128)S(1)} fusion(bf16[16,3,88,1408]{3,2,1,0:T(8,128)(2,1)} %bitcast.127, f32[1408]{0:T(1024)S(1)} %convert_element_type.80, f32[192]{0:T(256)S(1)} %add_rsqrt_fusion.1, f32[192]{0:T(256)S(1)} %broadcast_multiply_fusion.3, bf16[1,192,1408]{2,1,0:T(8,128)(2,1)S(1)} %copy-done.1, ...), kind=kOutput, calls=%fused_computation.39 | convolution fusion | flops 2285420544 | bytes 15689664 | tf_op jit(solution)/shard_map/dot_general | solution.py:116
  113.8 2.1 fusion.13
  117.6 5.2 %all-to-all-start = ((bf16[192,16,1,264]{0,3,2,1:T(8,128)(2,1)}), bf16[192,16,1,264]{0,3,2,1:T(8,128)(2,1)}, u32[]{:S(2)}, u32[]{:S(2)}) async-start(bf16[192,16,1,264]{0,3,2,1:T(8,128)(2,1)} %pad_maximum_fusion), calls=%async_computation | async-start | bytes 4325376 | tf_op jit(solution)/shard_map/all_to_all | solution.py:124
  122.8 40.6 %all-gather = s32[16,192,3]{1,2,0:T(4,128)S(1)} all-gather(s32[1,192,3]{1,2,0:T(4,128)S(1)} %add_bitcast_fusion), channel_id=1, replica_groups=mesh['seq'=16,'pack'=16] {'seq'}, dimensions={0}, use_global_device_ids=true | all-gather | bytes 39168 | tf_op jit(solution)/shard_map/all_gather | solution.py:113
  163.5 3.4 copy.64
  166.9 4.5 %squeeze.20 = bf16[3072,1,264]{0,2,1:T(8,128)(2,1)} reshape(bf16[16,192,1,1,264]{1,0,4,3,2:T(8,128)(2,1)} %copy.64) | data formatting | bytes 3244032 | tf_op jit(solution)/shard_map/squeeze | solution.py:124
  171.5 2.5 fusion.30
  174.7 32.9 %while.10 = (s32[]{:T(128)}, bf16[6,512,1,88]{1,3,2,0:T(8,128)(2,1)}, s32[6,512]{1,0:T(8,128)S(1)}, s32[1,3072]{1,0:T(1,128)S(1)}, bf16[6,512,1,88]{1,3,2,0:T(8,...) while((s32[]{:T(128)}, bf16[6,512,1,88]{1,3,2,0:T(8,128)(2,1)}, ...), condition=%wide.region_9.10_spmd, body=%wide.region_6.9_spmd.sunk | while | flops 567847936 | bytes 22328436 | solution.py:67
  174.8 2.3 fusion.43
  180.2 2.3 fusion.43
  185.7 2.3 fusion.43
  191.2 2.3 fusion.43
  196.7 2.3 fusion.43
  202.2 2.3 fusion.43
  207.7 2.2 copy.72
  209.9 5.5 %reshape.434 = bf16[3072,1,1,88]{3,2,1,0:T(2,128)(2,1)} reshape(bf16[6,512,1,88]{3,1,0,2:T(8,128)(2,1)} %copy.72) | data formatting | bytes 1081344 | tf_op jit(solution)/shard_map/broadcast_in_dim;reshape | solution.py:126
  216.0 18.9 %reduce.10 = bf16[3072,88]{1,0:T(8,128)(2,1)} reduce(bf16[3072,1,1,88]{3,2,1,0:T(2,128)(2,1)} %reshape.434, bf16[]{:T(256)} %broadcast.284), dimensions={1,2}, to_apply=%reshape.434.reduce_sub_computation | reduce | bytes 1081346 | tf_op jit(solution)/shard_map/broadcast_in_dim;reshape | solution.py:126
  234.8 3.8 reshape.443
  238.6 4.2 all-to-all-start.1
  242.9 9.0 %all-to-all-done.1 = bf16[16,2,8448]{2,1,0:T(2,128)(2,1)} async-done(((bf16[16,2,8448]{2,1,0:T(2,128)(2,1)}), bf16[16,2,8448]{2,1,0:T(2,128)(2,1)}, u32[]{:S(2)}, u32[]{:S(2)}) %all-to-all-start.1) | async-done | bytes 540704 | tf_op jit(solution)/shard_map/all_to_all | solution.py:126
  251.9 6.3 %reshape.444 = bf16[3072,1,1,88]{3,2,1,0:T(2,128)(2,1)} reshape(bf16[16,2,8448]{2,1,0:T(2,128)(2,1)} %all-to-all-done.1) | data formatting | bytes 1081344
  258.2 4.1 copy.68
  262.4 2.6 all_to_all.29
  265.0 3.3 copy.69
  268.3 2.6 reshape.421
  270.9 3.5 fusion.32
  277.0 80.0 %all-gather.6.cloned.1.call-done = bf16[768,5632]{1,0:T(8,128)(2,1)} async-done(((bf16[48,5632]{1,0:T(8,128)(2,1)}), bf16[768,5632]{1,0:T(8,128)(2,1)}) %all-gather.6.cloned.1.call-update) | async-done | bytes 8650768 | tf_op jit(solution)/shard_map/all_gather | solution.py:134
  357.0 6.1 %fusion.14 = bf16[768,224]{0,1:T(8,128)(2,1)S(1)} fusion(bf16[768,5632]{1,0:T(8,128)(2,1)} %all-gather.6.cloned.1.call-done, bf16[5632,224]{0,1:T(8,128)(2,1)S(1)} %copy-done, f32[224]{0:T(256)S(1)} %convert_element_type.89), kind=kOutput, calls=%fused_computation.30 | convolution fusion | flops 1938112512 | bytes 11518848 | tf_op jit(solution)/shard_map/dot_general | solution.py:133
  363.3 13.0 %gather_fusion = bf16[3072,224]{1,0:T(8,128)(2,1)} fusion(bf16[768,224]{1,0:T(8,128)(2,1)S(1)} %copy.70, s32[3072]{0:T(1024)S(1)} %broadcast_clamp_fusion), kind=kCustom, calls=%fused_computation | custom fusion | bytes 2764800 | tf_op jit(solution)/shard_map/jit(_take)/gather | solution.py:85
  376.4 3.0 select_select_fusion
  379.3 47.3 %all_to_all.35 = bf16[16,192,224]{2,1,0:T(8,128)(2,1)S(1)} all-to-all(bf16[16,192,224]{2,1,0:T(8,128)(2,1)S(1)} %select_select_fusion), channel_id=1, replica_groups=mesh['seq'=16,'pack'=16] {'pack'}, dimensions={0} | all-to-all | bytes 2752512 | tf_op jit(solution)/shard_map/all_to_all | solution.py:143
  (106 shorter events, 31.6 us)
Async XLA Ops:
  6.5 350.5 %copy-start = (bf16[5632,224]{0,1:T(8,128)(2,1)S(1)}, bf16[5632,224]{0,1:T(8,128)(2,1)}, u32[]{:S(2)}) copy-start(bf16[5632,224]{0,1:T(8,128)(2,1)} %param.25) | copy-start | bytes 7569412
  6.5 3.2 copy-start.9
  6.5 3.2 copy-start.1
  6.5 3.2 copy-start.3
  6.5 98.4 %all-gather.4.cloned.1.call-start = ((), (), s32[]{:S(2)}) async-start(), calls=%async_computation.3 | async-start | bytes 12638208 | tf_op jit(solution)/shard_map/all_gather | solution.py:118
  117.6 5.2 %copy-start.5 = (s32[1,192]{1,0:T(1,128)S(1)}, s32[1,192]{1,0:T(1,128)}, u32[]{:S(2)}) copy-start(s32[1,192]{1,0:T(1,128)} %param.22) | copy-start | bytes 2308
  117.6 5.2 %copy-start.6 = (s32[1,192]{1,0:T(1,128)S(1)}, s32[1,192]{1,0:T(1,128)}, u32[]{:S(2)}) copy-start(s32[1,192]{1,0:T(1,128)} %param.21) | copy-start | bytes 2308
  117.6 5.2 %copy-start.7 = (s32[1,192]{1,0:T(1,128)S(1)}, s32[1,192]{1,0:T(1,128)}, u32[]{:S(2)}) copy-start(s32[1,192]{1,0:T(1,128)} %param.20) | copy-start | bytes 2308
  117.6 46.0 %all-to-all-start = ((bf16[192,16,1,264]{0,3,2,1:T(8,128)(2,1)}), bf16[192,16,1,264]{0,3,2,1:T(8,128)(2,1)}, u32[]{:S(2)}, u32[]{:S(2)}) async-start(bf16[192,16,1,264]{0,3,2,1:T(8,128)(2,1)} %pad_maximum_fusion), calls=%async_computation | async-start | bytes 4325376 | tf_op jit(solution)/shard_map/all_to_all | solution.py:124
  177.1 1.1 copy-start.2
  182.6 1.1 copy-start.2
  188.1 1.1 copy-start.2
  193.6 1.1 copy-start.2
  199.0 1.1 copy-start.2
  204.5 1.1 copy-start.2
  234.8 8.1 %copy-start.4 = (bf16[1408]{0:T(1024)(128)(2,1)S(1)}, bf16[1408]{0:T(1024)(128)(2,1)}, u32[]{:S(2)}) copy-start(bf16[1408]{0:T(1024)(128)(2,1)} %param.24) | copy-start | bytes 8452
  238.6 13.3 %all-to-all-start.1 = ((bf16[16,2,8448]{2,1,0:T(2,128)(2,1)}), bf16[16,2,8448]{2,1,0:T(2,128)(2,1)}, u32[]{:S(2)}, u32[]{:S(2)}) async-start(bf16[16,2,8448]{2,1,0:T(2,128)(2,1)} %reshape.443), calls=%async_computation.1 | async-start | bytes 1081344 | tf_op jit(solution)/shard_map/all_to_all | solution.py:126
  242.9 114.1 %all-gather.6.cloned.1.call-start = ((), (), s32[]{:S(2)}) async-start(), calls=%async_computation.4 | async-start | bytes 9191424 | tf_op jit(solution)/shard_map/all_gather | solution.py:134
  274.6 1.4 copy-start.10
  274.6 2.0 copy-start.8
Sparse Core Ops, SparseCore 0:
  9.8 95.1 all-gather.3
  276.2 80.7 all-gather.5
where the time goes:
time: 436 us; the launch traced here: 435 us
  waiting for transfers between devices  184 us (42%)
  blocking collectives  87.9 us (20%)
  local copies, waits for them, and re-layouts  59.9 us (14%)
  matrix products  43.1 us (10%)
  other arithmetic  36.2 us (8%)
  between operations  13.8 us (3%)
  starting transfers between devices  9.46 us (2%)
    all_gather x1, waiting for transfers between devices, local(): lax.all_gather(qkv_weight, 'seq', axis=1, tiled=True)  94.6 us
    all_gather x1, waiting for transfers between devices, local(): lax.all_gather(merged, 'seq', axis=0, tiled=True)  80 us
    all_to_all x1, blocking collectives, local(): lax.all_to_all(outgoing, 'pack', split_axis=0, concat_axis=0, tiled=True)  47.3 us
    all_gather x1, blocking collectives, local(): lax.all_gather(jnp.stack([segment_ids[0], patch_rows[0], patch_column[0]]...  40.6 us
    another operation x1, other arithmetic, local(): result[:, None]  18.9 us
    dot_general x6, matrix products, one_block(): jnp.einsum('qhd,khd->hqk', queries_here, key_part, preferred_element_type...  14.1 us
    gather x1, local copies, waits for them, and re-layouts, route(): jnp.take(projected, source_rows.reshape(-1), axis=0)  13 us
    dot_general x6, matrix products, one_block(): jnp.einsum('hqk,khd->qhd', probs, value_part, preferred_element_type=jnp....  12.5 us
  transfers between devices with their start and end apart: 4, of which 3 were waited for; matrix products, arithmetic and copies ran while one was open for 1% of the time, Pallas kernels for 0%

commit v1 on v0

v1 whole, which is shorter than its diff:
```python
import functools

import jax
import jax.numpy as jnp
from jax import lax
from jax.experimental import pallas as pl
from jax.experimental.pallas import tpu as pltpu
from jax.sharding import PartitionSpec as P

D = 1408
HEADS = 16
HD = 88
ROWS = 192
GROUPS = 48
OUTC = 224
MOST = 192
EPSILON = 1e-06
F32 = jnp.float32
BF16 = jnp.bfloat16
MESH = pl.DeviceIdType.MESH
NT = (((1,), (1,)), ((), ()))
VM = pl.BlockSpec(memory_space=pltpu.VMEM)
SM = pl.BlockSpec(memory_space=pltpu.SMEM)


def iota(shape, axis):
    return lax.broadcasted_iota(jnp.int32, shape, axis)


def column_of(row):
    n = row.shape[1]
    eye = (iota((n, n), 0) == iota((n, n), 1)).astype(BF16)
    wide = jnp.broadcast_to(row, (8, n)).astype(BF16)
    return lax.dot_general(eye, wide, NT, preferred_element_type=F32)[:, :1]


def side_by_side(left, right):
    n = left.shape[1]
    first = (iota((n, 2 * n), 0) == iota((n, 2 * n), 1)).astype(BF16)
    second = (iota((n, 2 * n), 0) + n == iota((n, 2 * n), 1)).astype(BF16)
    return jnp.dot(left.astype(BF16), first, preferred_element_type=F32) + jnp.dot(
        right.astype(BF16), second, preferred_element_type=F32
    )


def layer_norm(values, gain):
    center = values - jnp.mean(values, axis=-1, keepdims=True)
    spread = jnp.mean(center * center, axis=-1, keepdims=True)
    return center * lax.rsqrt(spread + EPSILON) * gain


def embedded(patches_ref, mask_ref, embed_ref):
    chosen = column_of(mask_ref[...].astype(F32))
    return jnp.where(
        chosen > 0.5, embed_ref[...].astype(F32), patches_ref[0].astype(F32)
    )


def qkv_kernel(
    patches_ref,
    mask_ref,
    embed_ref,
    gain_ref,
    weight_ref,
    seg_ref,
    row_ref,
    col_ref,
    out_ref,
    labels_ref,
    tok,
    wts,
    prod,
    relay,
    mine,
    t_send,
    t_recv,
    w_send,
    w_recv,
    p_send,
    p_recv,
    m_send,
    m_recv,
):
    s = lax.axis_index("seq")
    core = lax.rem(lax.axis_index("pack"), 2)
    y, x = s // 4, lax.rem(s, 4)
    a = x * (1 - core) + y * core
    b = y * (1 - core) + x * core
    step_a, step_b = 1 + 3 * core, 4 - 3 * core

    def on_a(k):
        return {"seq": lax.rem(a + k, 4) * step_a + b * step_b}

    def on_b(k):
        return {"seq": a * step_a + lax.rem(b + k, 4) * step_b}

    barrier = pltpu.get_barrier_semaphore()
    for d in range(1, 16):
        pl.semaphore_signal(
            barrier, inc=1, device_id={"seq": lax.rem(s + d, 16)}, device_id_type=MESH
        )

    mine[0:1, :] = seg_ref[...]
    mine[1:2, :] = row_ref[...]
    mine[2:3, :] = col_ref[...]
    mine[3:8, :] = jnp.zeros((5, ROWS), jnp.int32)
    labels_ref[s] = mine[...]
    inputs = embedded(patches_ref, mask_ref, embed_ref)
    tok[a] = layer_norm(inputs, gain_ref[...].astype(F32)).astype(BF16)
    wts[b] = weight_ref[...]
    pl.semaphore_wait(barrier, 15)

    def copy(src, dst, send, recv, k, where):
        return pltpu.make_async_remote_copy(
            src_ref=src,
            dst_ref=dst,
            send_sem=send.at[k],
            recv_sem=recv.at[k],
            device_id=where,
            device_id_type=MESH,
        )

    def ring(buf, pos, cut, size, send, recv, to):
        upper, lower = pl.ds(0, cut), pl.ds(cut, size - cut)
        before, after = lax.rem(pos + 3, 4), lax.rem(pos + 1, 4)

        def one(slot, part, k, where):
            ref = buf.at[slot, part]
            return copy(ref, ref, send, recv, k, where)

        return [
            one(pos, upper, 0, to(1)),
            one(pos, lower, 1, to(3)),
            one(pos, lower, 2, to(1)),
            one(pos, upper, 3, to(3)),
            one(before, upper, 4, to(1)),
            one(after, lower, 5, to(3)),
        ]

    w_ring = ring(wts, b, 136, 264, w_send, w_recv, on_b)
    t_ring = ring(tok, a, 96, ROWS, t_send, t_recv, on_a)
    for k in range(4):
        w_ring[k].start()
        t_ring[k].start()
    labels = []
    for d in range(1, 16):
        labels.append(
            copy(mine, labels_ref.at[s], m_send, m_recv, d, {"seq": lax.rem(s + d, 16)})
        )
        labels[-1].start()
    for one in labels:
        one.wait_recv()

    feature = iota((HD, 1), 0)
    quarter = HD // 4
    place = lax.rem(feature, quarter).astype(F32)
    frequency = jnp.exp(place * (-9.210340371976184 / quarter))
    is_row = feature < 2 * quarter
    is_first = lax.rem(feature, 2 * quarter) < quarter

    def table(pair):
        left = labels_ref[(2 * pair) * step_a + b * step_b].astype(F32)
        right = labels_ref[(2 * pair + 1) * step_a + b * step_b].astype(F32)
        both = side_by_side(left, right)
        angle = jnp.where(is_row, both[1:2], both[2:3]) * frequency
        sine = jnp.sin(angle)
        return jnp.cos(angle), jnp.where(is_first, -sine, 0.0), jnp.where(is_first, 0.0, sine)

    pairs = (a // 2, 1 - a // 2)
    tables = [table(pair) for pair in pairs]

    t_ring[0].wait_recv()
    t_ring[4].start()
    t_ring[1].wait_recv()
    t_ring[5].start()
    w_ring[0].wait_recv()
    w_ring[4].start()
    w_ring[1].wait_recv()
    w_ring[5].start()
    t_ring[2].wait_recv()
    t_ring[3].wait_recv()
    w_ring[2].wait_recv()
    w_ring[3].wait_recv()

    def turn(part, k):
        cosine, ahead, behind = tables[k]
        return (
            part * cosine
            + pltpu.roll(part, HD - quarter, 0) * ahead
            + pltpu.roll(part, quarter, 0) * behind
        )

    def block(k, head):
        tokens = tok[pl.ds(2 * pairs[k], 2)].reshape(2 * ROWS, D)
        projected = lax.dot_general(wts[head], tokens, NT, preferred_element_type=F32)
        return jnp.concatenate(
            [turn(projected[:HD], k), turn(projected[HD : 2 * HD], k), projected[2 * HD :]],
            axis=0,
        ).astype(BF16)

    up, down, far = lax.rem(b + 1, 4), lax.rem(b + 3, 4), lax.rem(b + 2, 4)
    sends = {}

    def send_to(k, head, n, where, slot):
        prod[slot] = block(k, head)
        sends[n] = copy(prod.at[slot], out_ref.at[b, pairs[k]], p_send, p_recv, n, where)
        sends[n].start()

    def send_far(k, n, where, slot):
        prod[slot] = block(k, far)
        sends[n] = copy(prod.at[slot], relay.at[k], p_send, p_recv, n, where)
        sends[n].start()

    send_to(0, up, 0, on_b(1), 0)
    send_to(0, down, 2, on_b(3), 1)
    w_ring[4].wait_recv()
    w_ring[5].wait_recv()
    send_far(0, 4, on_b(1), 2)
    t_ring[4].wait_recv()
    t_ring[5].wait_recv()
    send_far(1, 5, on_b(3), 3)
    send_to(1, up, 1, on_b(1), 4)
    send_to(1, down, 3, on_b(3), 5)
    out_ref[b, pairs[0]] = block(0, b)
    sends[4].wait_recv()
    sends[6] = copy(relay.at[0], out_ref.at[down, pairs[0]], p_send, p_recv, 6, on_b(1))
    sends[6].start()
    sends[5].wait_recv()
    sends[7] = copy(relay.at[1], out_ref.at[up, pairs[1]], p_send, p_recv, 7, on_b(3))
    sends[7].start()
    out_ref[b, pairs[1]] = block(1, b)
    for n in (0, 1, 2, 3, 6, 7):
        sends[n].wait_recv()
    for one in w_ring + t_ring + labels + list(sends.values()):
        one.wait_send()


def attention_kernel(n_pack, qkv_ref, labels_ref, owner_ref, out_ref, table_ref, qs, kvs, segs):
    core = lax.rem(lax.axis_index("pack"), 2)
    half = ROWS
    wide = 2 * ROWS

    @pl.when(core == 0)
    def _():
        for m in range(8):
            kvs[m] = qkv_ref[m // 2, m % 2]

    @pl.when(core == 1)
    def _():
        lane = iota((3 * HD, wide), 1)
        for m in range(8):
            second, j = (m // 2) % 2, m // 4
            left = qkv_ref[2 * (m % 2), j].astype(F32)
            right = qkv_ref[2 * (m % 2) + 1, j].astype(F32)
            if second:
                left = pltpu.roll(left, half, 1)
            else:
                right = pltpu.roll(right, half, 1)
            kvs[m] = jnp.where(lane < half, left, right).astype(BF16)

    for m in range(8):
        turned = jnp.concatenate(
            [kvs[m].astype(F32)[:HD], jnp.zeros((128 - HD, wide), F32)], axis=0
        ).T
        qs[2 * m] = turned[:half].astype(BF16)
        qs[2 * m + 1] = turned[half:].astype(BF16)
        segs[m] = side_by_side(
            labels_ref[2 * m].astype(F32), labels_ref[2 * m + 1].astype(F32)
        )

    every = jnp.concatenate([labels_ref[k][0:1] for k in range(16)], axis=0)
    total = 16 * ROWS
    starts = [jnp.int32(0)]
    for image in range(1, 8):
        starts.append(jnp.sum((every < image).astype(jnp.int32)))
    starts.append(jnp.int32(total))
    lane = iota((1, 128), 1)
    first = jnp.zeros((1, 128), jnp.int32)
    length = jnp.zeros((1, 128), jnp.int32)
    for image in range(8):
        mine = lane == owner_ref[0, image]
        first = jnp.where(mine, starts[image] // 4, first)
        length = jnp.where(mine, (starts[image + 1] - starts[image]) // 4, length)
    table_ref[0:1, :] = first
    table_ref[1:2, :] = length
    table_ref[2:8, :] = jnp.zeros((6, 128), jnp.int32)

    scale = HD ** (-0.5) * 1.4426950408889634
    low = -0.7 * 3.4028235e38

    def one_block(s, carry):
        begin = jnp.int32(0)
        end = jnp.int32(total)
        for image in range(1, 8):
            begin = jnp.where(starts[image] <= s * ROWS, starts[image], begin)
        for image in range(7, 0, -1):
            end = jnp.where(starts[image] >= (s + 1) * ROWS, starts[image], end)
        queries = qs[s][:, :HD]
        own = column_of(labels_ref[s][0:1].astype(F32))

        def one_step(m, state):
            top, denominator, acc = state
            scores = jnp.dot(queries, kvs[m, pl.ds(HD, HD)], preferred_element_type=F32)
            scores = jnp.where(own == segs[m][0:1], scores, low)
            new_top = jnp.maximum(top, jnp.max(scores, axis=-1, keepdims=True))
            shrink = jnp.exp2((top - new_top) * scale)
            weights = jnp.exp2((scores - new_top) * scale)
            denominator = denominator * shrink + jnp.sum(weights, axis=-1, keepdims=True)
            acc = acc * shrink + lax.dot_general(
                weights.astype(BF16), kvs[m, pl.ds(2 * HD, HD)], NT, preferred_element_type=F32
            )
            return new_top, denominator, acc

        state = (
            jnp.full((ROWS, 1), low, F32),
            jnp.zeros((ROWS, 1), F32),
            jnp.zeros((ROWS, HD), F32),
        )
        _, denominator, acc = lax.fori_loop(
            begin // wide, (end + wide - 1) // wide, one_step, state
        )
        out_ref[s] = (acc / denominator).astype(BF16)
        return carry

    lax.fori_loop(0, 16, one_block, 0)


def merge_kernel(
    n_pack,
    att_ref,
    patches_ref,
    mask_ref,
    embed_ref,
    wo_ref,
    gain_ref,
    wm_ref,
    bias_ref,
    table_ref,
    rows_ref,
    tables_ref,
    heads,
    acc,
    tiles,
    mg,
    h_send,
    h_recv,
    g_send,
    g_recv,
    z_send,
    z_recv,
    c_send,
    c_recv,
    b_send,
    b_recv,
):
    s = lax.axis_index("seq")
    p = lax.axis_index("pack")
    nz = n_pack // 2
    z, core = p // 2, lax.rem(p, 2)
    y, x = s // 4, lax.rem(s, 4)

    barrier = pltpu.get_barrier_semaphore()
    for d in range(1, 16):
        pl.semaphore_signal(
            barrier, inc=1, device_id={"seq": lax.rem(s + d, 16)}, device_id_type=MESH
        )
    for d in range(1, n_pack):
        pl.semaphore_signal(
            barrier, inc=1, device_id={"pack": lax.rem(p + d, n_pack)}, device_id_type=MESH
        )
    pl.semaphore_wait(barrier, 15 + n_pack - 1)

    def copy(src, dst, send, recv, k, where):
        return pltpu.make_async_remote_copy(
            src_ref=src,
            dst_ref=dst,
            send_sem=send.at[k],
            recv_sem=recv.at[k],
            device_id=where,
            device_id_type=MESH,
        )

    out = []
    back = []
    for d in range(1, 16):
        to = lax.rem(s + d, 16)
        back.append(copy(att_ref.at[to], heads.at[s], h_send, h_recv, d, {"seq": to}))
        back[-1].start()
    tabs = []
    for d in range(1, n_pack):
        tabs.append(
            copy(table_ref, tables_ref.at[p], b_send, b_recv, d, {"pack": lax.rem(p + d, n_pack)})
        )
        tabs[-1].start()
    tables_ref[p] = table_ref[...]
    out += back + tabs
    inputs = embedded(patches_ref, mask_ref, embed_ref)
    acc[...] = inputs + jnp.dot(att_ref[s], wo_ref[s], preferred_element_type=F32)
    for d in range(1, 16):
        back[d - 1].wait_recv()
        head = lax.rem(s + 16 - d, 16)
        acc[...] += jnp.dot(heads[head], wo_ref[head], preferred_element_type=F32)
    normed = layer_norm(acc[...], gain_ref[...].astype(F32))
    for t in range(D // 128):
        tiles[t] = normed[:, 128 * t : 128 * (t + 1)]
    for t in range(D // 128):
        for j in range(4):
            mg[s, j, :, 128 * t : 128 * (t + 1)] = tiles[t, pl.ds(j, GROUPS, stride=4), :].astype(
                BF16
            )

    order = {0: 0, -1: 1, 1: 2, 2: 3}

    def device(half, df, dg):
        dx, dy = (df, dg) if half == 0 else (dg, df)
        return lax.rem(y + dy + 4, 4) * 4 + lax.rem(x + dx + 4, 4)

    started = {}

    def send(half, phase, df, dg, kind):
        k = ((half * 2 + phase) * 4 + (order[df] if phase else 0)) * 4 + kind
        blk = device(half, df, dg)
        step = 1 if kind in (0, 2) else -1
        to = device(half, 0, step) if phase else device(half, step, 0)
        if kind < 2:
            ref = mg.at[blk, pl.ds(2 * half, 2)]
        else:
            ref = mg.at[blk, pl.ds(2 * half + kind - 2, 1)]
        one = copy(ref, ref, g_send, g_recv, k, {"seq": to})
        one.start()
        started[half, phase, order[df] if phase else 0, kind] = one
        out.append(one)

    def arrive(half, df, dg):
        phase = 0 if dg == 0 else 1
        off = df if phase == 0 else dg
        k = order[df] if phase else 0
        if off == 2:
            started[half, phase, k, 2].wait_recv()
            started[half, phase, k, 3].wait_recv()
        elif off == -1:
            started[half, phase, k, 0].wait_recv()
            send(half, phase, df, dg, 2)
        else:
            started[half, phase, k, 1].wait_recv()
            send(half, phase, df, dg, 3)
        if phase == 0:
            send(half, 1, df, 0, 0)
            send(half, 1, df, 0, 1)

    done = set()

    def need(half, df, dg):
        if (half, df, dg) not in done and (df, dg) != (0, 0):
            done.add((half, df, dg))
            arrive(half, df, dg)

    z_out = {}

    def z_copy(ref, k, step, c):
        if step == 2:
            return copy(ref, ref, c_send, c_recv, c * nz + k, {"pack": z * 2 + 1 - core})
        to = lax.rem(z + step + nz, nz) * 2 + core
        return copy(ref, ref, z_send, z_recv, (c * 2 + (step + 1) // 2) * nz + k, {"pack": to})

    def chunk(c, dy):
        row = lax.rem(y + dy + 4, 4)
        total = jnp.broadcast_to(bias_ref[...].astype(F32), (4 * GROUPS, OUTC))
        for j in range(4):
            part = mg[pl.ds(4 * row, 4), j].reshape(4 * GROUPS, D)
            total += lax.dot_general(
                part, wm_ref[:, pl.ds(j * D, D)], NT, preferred_element_type=F32
            )
        rows_ref[p, row] = total.astype(BF16)
        own = rows_ref.at[p, row]
        for step in (1, -1, 2):
            z_out[c, step, 0] = z_copy(own, 0, step, c)
            z_out[c, step, 0].start()

    def hops(c):
        return (nz // 2, nz - 1 - nz // 2) if c % 2 == 0 else (nz - 1 - nz // 2, nz // 2)

    def pass_on(c, dy):
        row = lax.rem(y + dy + 4, 4)
        limits = hops(c)
        for h in range(1, max(limits) + 1):
            for step, limit in ((1, limits[0]), (-1, limits[1])):
                if h > limit:
                    continue
                z_out[c, step, h - 1].wait_recv()
                pack = lax.rem(z - step * h + nz, nz) * 2 + core
                ref = rows_ref.at[pack, row]
                if h < limit:
                    z_out[c, step, h] = z_copy(ref, h, step, c)
                    z_out[c, step, h].start()
                k = h if step == 1 else limits[0] + h
                z_out[c, 2, k] = z_copy(ref, k, 2, c)
                z_out[c, 2, k].start()

    for half in range(2):
        send(half, 0, 0, 0, 0)
        send(half, 0, 0, 0, 1)
    for half in range(2):
        send(half, 1, 0, 0, 0)
        send(half, 1, 0, 0, 1)
    for half in range(2):
        need(half, -1, 0)
        need(half, 1, 0)
    for half in range(2):
        need(half, 0, -1)
        need(half, 0, 1)
    for half in range(2):
        need(half, 2, 0)

    def row_ready(dy):
        for dx in (0, -1, 1, 2):
            need(0, dx, dy)
            need(1, dy, dx)

    row_ready(0)
    chunk(0, 0)
    for df in (-1, 1, 2):
        for dg in (-1, 1):
            for half in range(2):
                need(half, df, dg)
    row_ready(-1)
    chunk(1, -1)
    pass_on(0, 0)
    row_ready(1)
    chunk(2, 1)
    pass_on(1, -1)
    row_ready(2)
    chunk(3, 2)
    pass_on(2, 1)
    pass_on(3, 2)
    for c in range(4):
        for k in range(nz):
            z_out[c, 2, k].wait_recv()
    for one in tabs:
        one.wait_recv()
    for one in out + list(z_out.values()):
        one.wait_send()


def select_kernel(n_pack, rows_ref, tables_ref, out_ref):
    p = lax.axis_index("pack")
    total = 4 * MOST
    window = MOST + 16
    for q in range(n_pack):
        mine = iota((1, 128), 1) == p
        first = jnp.sum(jnp.where(mine, tables_ref[q, 0:1, :], 0))
        length = jnp.sum(jnp.where(mine, tables_ref[q, 1:2, :], 0))
        base = pl.multiple_of(jnp.minimum((first // 16) * 16, total - window), 16)
        slot = iota((MOST, window), 0)
        source = iota((MOST, window), 1)
        pick = ((source == slot + (first - base)) & (slot < length)).astype(BF16)
        out_ref[0, q] = jnp.dot(
            pick, rows_ref[q, pl.ds(base, window)], preferred_element_type=F32
        ).astype(BF16)


def local(
    patches,
    patch_mask,
    mask_embed,
    norm_gain,
    qkv_weight,
    segment_ids,
    patch_rows,
    patch_column,
    out_weight,
    merge_gain,
    merge_weight,
    merge_bias,
    image_owner,
):
    n_pack = lax.axis_size("pack")
    nz = n_pack // 2
    dma = pltpu.SemaphoreType.DMA
    shape = jax.ShapeDtypeStruct
    embed = mask_embed[None, :]
    qkv, labels = pl.pallas_call(
        qkv_kernel,
        out_shape=(shape((4, 2, 3 * HD, 2 * ROWS), BF16), shape((16, 8, ROWS), jnp.int32)),
        in_specs=[VM] * 8,
        out_specs=(VM, VM),
        scratch_shapes=[
            pltpu.VMEM((4, ROWS, D), BF16),
            pltpu.VMEM((4, 3 * HD, D), BF16),
            pltpu.VMEM((6, 3 * HD, 2 * ROWS), BF16),
            pltpu.VMEM((2, 3 * HD, 2 * ROWS), BF16),
            pltpu.VMEM((8, ROWS), jnp.int32),
            dma((6,)),
            dma((6,)),
            dma((6,)),
            dma((6,)),
            dma((8,)),
            dma((8,)),
            dma((16,)),
            dma((16,)),
        ],
        compiler_params=pltpu.CompilerParams(
            collective_id=0, has_side_effects=True, vmem_limit_bytes=60 * 2**20
        ),
        name="qkv",
    )(
        patches,
        patch_mask,
        embed,
        norm_gain[None, :],
        qkv_weight.T,
        segment_ids,
        patch_rows,
        patch_column,
    )
    attended, table = pl.pallas_call(
        functools.partial(attention_kernel, n_pack),
        out_shape=(shape((16, ROWS, HD), BF16), shape((8, 128), jnp.int32)),
        in_specs=[VM, VM, SM],
        out_specs=(VM, VM),
        scratch_shapes=[
            pltpu.VMEM((16, ROWS, 128), BF16),
            pltpu.VMEM((8, 3 * HD, 2 * ROWS), BF16),
            pltpu.VMEM((8, 8, 2 * ROWS), F32),
        ],
        compiler_params=pltpu.CompilerParams(vmem_limit_bytes=60 * 2**20),
        name="attention",
    )(qkv, labels, image_owner)
    rows, tables = pl.pallas_call(
        functools.partial(merge_kernel, n_pack),
        out_shape=(
            shape((n_pack, 4, 4 * GROUPS, OUTC), BF16),
            shape((n_pack, 8, 128), jnp.int32),
        ),
        in_specs=[VM] * 9,
        out_specs=(VM, VM),
        scratch_shapes=[
            pltpu.VMEM((16, ROWS, HD), BF16),
            pltpu.VMEM((ROWS, D), F32),
            pltpu.VMEM((D // 128, ROWS, 128), F32),
            pltpu.VMEM((16, 4, GROUPS, D), BF16),
            dma((16,)),
            dma((16,)),
            dma((64,)),
            dma((64,)),
            dma((8 * nz,)),
            dma((8 * nz,)),
            dma((4 * nz,)),
            dma((4 * nz,)),
            dma((n_pack,)),
            dma((n_pack,)),
        ],
        compiler_params=pltpu.CompilerParams(
            collective_id=1, has_side_effects=True, vmem_limit_bytes=60 * 2**20
        ),
        name="merge",
    )(
        attended,
        patches,
        patch_mask,
        embed,
        out_weight.reshape(HEADS, HD, D),
        merge_gain[None, :],
        merge_weight.T,
        merge_bias[None, :],
        table,
    )
    return pl.pallas_call(
        functools.partial(select_kernel, n_pack),
        out_shape=shape((1, n_pack, MOST, OUTC), BF16),
        in_specs=[VM, VM],
        out_specs=VM,
        compiler_params=pltpu.CompilerParams(vmem_limit_bytes=60 * 2**20),
        name="select",
    )(rows.reshape(n_pack, 4 * MOST, OUTC), tables)


def solution(mesh):
    placed = (
        P("pack", "seq", None),
        P("pack", "seq"),
        P(),
        P(),
        P(None, "seq"),
        P("pack", "seq"),
        P("pack", "seq"),
        P("pack", "seq"),
        P(),
        P(),
        P(None, "seq"),
        P("seq"),
        P("pack", None),
    )
    return jax.shard_map(
        local, mesh=mesh, in_specs=placed, out_specs=P("pack", None, None, "seq"), check_vma=False
    )
```

time: 436 us -> 214 us (0.49)
  Pallas kernels: 0 us -> 209 us
  waiting for transfers between devices: 184 us -> 0 us
  blocking collectives: 87.9 us -> 0 us
  local copies, waits for them, and re-layouts: 59.9 us -> 5.02 us
  matrix products: 43.1 us -> 0 us
  other arithmetic: 36.2 us -> 0 us
  between operations: 13.8 us -> 0.02 us
  starting transfers between devices: 9.46 us -> 0 us
    pallas_call x0 -> x4, Pallas kernels: none -> 209 us  [the longest x1 132 us: local(): pl.pallas_call(functools.partial(merge_kernel, n_pack), out_shape=(shape(...]
    all_gather x2 -> x0, waiting for transfers between devices: 175 us -> none  [the longest x1 94.6 us: local(): lax.all_gather(qkv_weight, 'seq', axis=1, tiled=True)]
    all_to_all x1 -> x0, blocking collectives: 47.3 us -> none  [local(): lax.all_to_all(outgoing, 'pack', split_axis=0, concat_axis=0, tiled=True)]
    dot_general x15 -> x0, matrix products: 43.1 us -> none  [the longest x6 14.1 us: one_block(): jnp.einsum('qhd,khd->hqk', queries_here, key_part, preferred_element_type...]
    all_gather x1 -> x0, blocking collectives: 40.6 us -> none  [local(): lax.all_gather(jnp.stack([segment_ids[0], patch_rows[0], patch_column[0]]...]
    another operation x5 -> x0, other arithmetic: 21.4 us -> none  [the longest x1 18.9 us: local(): result[:, None]]
    all_to_all x4 -> x0, local copies, waits for them, and re-layouts: 13.4 us -> none  [the longest x3 10 us: local(): lax.all_to_all(result[:, None], 'seq', split_axis=0, concat_axis=1, tiled...]
    gather x1 -> x0, local copies, waits for them, and re-layouts: 13 us -> none  [route(): jnp.take(projected, source_rows.reshape(-1), axis=0)]
  transfers between devices with their start and end apart: 4 -> 0, of which waited for: 3 -> 0; matrix products, arithmetic and copies ran while one was open for 1% -> 0% of each run, Pallas kernels for 0% -> 0%
where the time goes in v1:
time: 214 us
  Pallas kernels  209 us (98%)
  local copies, waits for them, and re-layouts  5.02 us (2%)
    pallas_call x1, Pallas kernels, local(): pl.pallas_call(functools.partial(merge_kernel, n_pack), out_shape=(shape(...  132 us
    pallas_call x1, Pallas kernels, local(): pl.pallas_call(qkv_kernel, out_shape=(shape((4, 2, 3 * HD, 2 * ROWS), BF1...  47.2 us
    pallas_call x1, Pallas kernels, local(): pl.pallas_call(functools.partial(attention_kernel, n_pack), out_shape=(sh...  24.8 us
    pallas_call x1, Pallas kernels, local(): pl.pallas_call(functools.partial(select_kernel, n_pack), out_shape=shape(...  4.82 us

profile of v1, /device:TPU:1, one launch (start us, length us, event | category | flops | bytes accessed | tf_op | source)
XLA Modules:
  0.0 214.2 jit_solution(17724155173127568153)
XLA Ops:
  0.0 1.2 broadcast_in_dim.15.bias_ref
  1.2 1.3 broadcast_in_dim.12.embed_ref
  2.5 1.3 broadcast_in_dim.13.gain_ref
  3.7 1.3 broadcast_in_dim.14.gain_ref
  5.0 47.2 %qkv.1 = (bf16[4,2,264,384]{3,2,1,0:T(8,128)(2,1)}, s32[16,8,192]{2,1,0:T(8,128)}) custom-call(bf16[1,192,1408]{2,1,0:T(8,128)(2,1)} %patches_ref.3, s32[1,192]{1,0:T(1,128)} %mask_ref.3, bf16[1,1408]{1,0:T(2,128)(2,1)} %broadcast_in_dim.12.embed_ref, bf16[1,1408]{1,0:T(2,128)(2,1)} %broadcast_in_dim.13.gain_ref, bf16[264,1408]{1,0:T(8,128)(2,1)} %bitcast.7, ...), custom_call_target="tpu_custom_call" | custom-call | tf_op jit(solution)/shard_map/qkv/pallas_call | solution.py:582
  52.2 24.8 %attention.1 = (bf16[16,192,88]{2,1,0:T(8,128)(2,1)}, s32[8,128]{1,0:T(8,128)}) custom-call(bf16[4,2,264,384]{3,2,1,0:T(8,128)(2,1)} %get-tuple-element.11.qkv_ref, s32[16,8,192]{2,1,0:T(8,128)} %get-tuple-element.12.labels_ref, s32[1,8]{1,0:T(1,128)} %owner_ref.1), custom_call_target="tpu_custom_call" | custom-call | tf_op jit(solution)/shard_map/attention/pallas_call | solution.py:616
  77.0 132.3 %merge.1 = (bf16[16,4,192,224]{3,2,1,0:T(8,128)(2,1)}, s32[16,8,128]{2,1,0:T(8,128)}) custom-call(bf16[16,192,88]{2,1,0:T(8,128)(2,1)} %get-tuple-element.13.att_ref, bf16[1,192,1408]{2,1,0:T(8,128)(2,1)} %patches_ref.3, s32[1,192]{1,0:T(1,128)} %mask_ref.3, bf16[1,1408]{1,0:T(2,128)(2,1)} %broadcast_in_dim.12.embed_ref, bf16[16,88,1408]{2,1,0:T(8,128)(2,1)} %bitcast.5, ...), custom_call_target="tpu_custom_call" | custom-call | tf_op jit(solution)/shard_map/merge/pallas_call | solution.py:629
  209.4 4.8 %select.1 = bf16[1,16,192,224]{3,2,1,0:T(8,128)(2,1)} custom-call(bf16[16,768,224]{2,1,0:T(8,128)(2,1)} %bitcast.4, s32[16,8,128]{2,1,0:T(8,128)} %get-tuple-element.16.tables_ref), custom_call_target="tpu_custom_call" | custom-call | tf_op jit(solution)/shard_map/select/pallas_call | solution.py:668

commit v2 on v1

--- a/solution.py
+++ b/solution.py
@@ -20,6 +20,7 @@
 MESH = pl.DeviceIdType.MESH
 NT = (((1,), (1,)), ((), ()))
 VM = pl.BlockSpec(memory_space=pltpu.VMEM)
+ANY = pl.BlockSpec(memory_space=pl.ANY)
 SM = pl.BlockSpec(memory_space=pltpu.SMEM)
 
 
@@ -52,8 +53,89 @@
 def embedded(patches_ref, mask_ref, embed_ref):
     chosen = column_of(mask_ref[...].astype(F32))
     return jnp.where(
-        chosen > 0.5, embed_ref[...].astype(F32), patches_ref[0].astype(F32)
-    )
+        chosen > 0.5, embed_ref[...].astype(F32).reshape(1, D), patches_ref[0].astype(F32)
+    )
+
+def remote(src, dst, send, recv, k, where):
+    return pltpu.make_async_remote_copy(
+        src_ref=src,
+        dst_ref=dst,
+        send_sem=send.at[k],
+        recv_sem=recv.at[k],
+        device_id=where,
+        device_id_type=MESH,
+    )
+
+
+def ring_of_four(own, ref_of, pos, parts, send, recv, to):
+    first, second = parts
+    before, after = lax.rem(pos + 3, 4), lax.rem(pos + 1, 4)
+
+    def fresh(part, k, where):
+        return remote(own(part), ref_of(pos, part), send, recv, k, where)
+
+    def again(slot, part, k, where):
+        ref = ref_of(slot, part)
+        return remote(ref, ref, send, recv, k, where)
+
+    return [
+        fresh(first, 0, to(1)),
+        fresh(second, 1, to(3)),
+        fresh(second, 2, to(1)),
+        fresh(first, 3, to(3)),
+        again(before, first, 4, to(1)),
+        again(after, second, 5, to(3)),
+    ]
+
+
+class PackRing:
+    def __init__(self, n_pack, ref_of, limits, sems, base, own=None):
+        self.p = lax.axis_index("pack")
+        self.nz = n_pack // 2
+        self.z, self.core = self.p // 2, lax.rem(self.p, 2)
+        self.ref_of, self.limits, self.sems, self.base, self.own = ref_of, limits, sems, base, own
+        self.made = {}
+
+    def go(self, pack, step, k, own=False):
+        z_send, z_recv, c_send, c_recv = self.sems
+        ref = self.ref_of(pack)
+        src = self.own if own and self.own is not None else ref
+        if step == 2:
+            to = self.z * 2 + 1 - self.core
+            one = remote(src, ref, c_send, c_recv, self.base * self.nz + k, {"pack": to})
+        else:
+            to = lax.rem(self.z + step + self.nz, self.nz) * 2 + self.core
+            n = (self.base * 2 + (step + 1) // 2) * self.nz + k
+            one = remote(src, ref, z_send, z_recv, n, {"pack": to})
+        one.start()
+        self.made[step, k] = one
+
+    def start(self):
+        for step in (1, -1, 2):
+            self.go(self.p, step, 0, own=True)
+
+    def hop(self, h):
+        for step, limit in ((1, self.limits[0]), (-1, self.limits[1])):
+            if h > limit:
+                continue
+            self.made[step, h - 1].wait_recv()
+            pack = lax.rem(self.z - step * h + self.nz, self.nz) * 2 + self.core
+            if h < limit:
+                self.go(pack, step, h)
+            self.go(pack, 2, h if step == 1 else self.limits[0] + h)
+
+    def finish(self):
+        for k in range(self.nz):
+            self.made[2, k].wait_recv()
+
+    def drain(self):
+        for one in self.made.values():
+            one.wait_send()
+
+
+def limits_of(nz, c):
+    low, high = nz - 1 - nz // 2, nz // 2
+    return (high, low) if c % 2 == 0 else (low, high)
 
 
 def qkv_kernel(
@@ -70,7 +152,6 @@
     tok,
     wts,
     prod,
-    relay,
     mine,
     t_send,
     t_recv,
@@ -95,60 +176,55 @@
         return {"seq": a * step_a + lax.rem(b + k, 4) * step_b}
 
     barrier = pltpu.get_barrier_semaphore()
+
+    def greet(where):
+        pl.semaphore_signal(barrier, inc=1, device_id=where, device_id_type=MESH)
+
     for d in range(1, 16):
-        pl.semaphore_signal(
-            barrier, inc=1, device_id={"seq": lax.rem(s + d, 16)}, device_id_type=MESH
-        )
+        greet({"seq": lax.rem(s + d, 16)})
 
     mine[0:1, :] = seg_ref[...]
     mine[1:2, :] = row_ref[...]
     mine[2:3, :] = col_ref[...]
     mine[3:8, :] = jnp.zeros((5, ROWS), jnp.int32)
     labels_ref[s] = mine[...]
+    pl.semaphore_wait(barrier, 15)
+
+    w_ring = ring_of_four(
+        lambda part: weight_ref.at[part],
+        lambda slot, part: wts.at[slot, part],
+        b,
+        (pl.ds(0, 136), pl.ds(136, 128)),
+        w_send,
+        w_recv,
+        on_b,
+    )
+    t_ring = ring_of_four(
+        lambda part: tok.at[a, part],
+        lambda slot, part: tok.at[slot, part],
+        a,
+        (pl.ds(0, 96), pl.ds(96, 96)),
+        t_send,
+        t_recv,
+        on_a,
+    )
+    w_ring[0].start()
+    w_ring[1].start()
+    small = []
+    for d in range(1, 16):
+        small.append(
+            remote(mine, labels_ref.at[s], m_send, m_recv, d, {"seq": lax.rem(s + d, 16)})
+        )
+    for one in small:
+        one.start()
+    w_ring[2].start()
+    w_ring[3].start()
     inputs = embedded(patches_ref, mask_ref, embed_ref)
-    tok[a] = layer_norm(inputs, gain_ref[...].astype(F32)).astype(BF16)
+    tok[a] = layer_norm(inputs, gain_ref[...].astype(F32).reshape(1, D)).astype(BF16)
+    for k in range(4):
+        t_ring[k].start()
     wts[b] = weight_ref[...]
-    pl.semaphore_wait(barrier, 15)
-
-    def copy(src, dst, send, recv, k, where):
-        return pltpu.make_async_remote_copy(
-            src_ref=src,
-            dst_ref=dst,
-            send_sem=send.at[k],
-            recv_sem=recv.at[k],
-            device_id=where,
-            device_id_type=MESH,
-        )
-
-    def ring(buf, pos, cut, size, send, recv, to):
-        upper, lower = pl.ds(0, cut), pl.ds(cut, size - cut)
-        before, after = lax.rem(pos + 3, 4), lax.rem(pos + 1, 4)
-
-        def one(slot, part, k, where):
-            ref = buf.at[slot, part]
-            return copy(ref, ref, send, recv, k, where)
-
-        return [
-            one(pos, upper, 0, to(1)),
-            one(pos, lower, 1, to(3)),
-            one(pos, lower, 2, to(1)),
-            one(pos, upper, 3, to(3)),
-            one(before, upper, 4, to(1)),
-            one(after, lower, 5, to(3)),
-        ]
-
-    w_ring = ring(wts, b, 136, 264, w_send, w_recv, on_b)
-    t_ring = ring(tok, a, 96, ROWS, t_send, t_recv, on_a)
-    for k in range(4):
-        w_ring[k].start()
-        t_ring[k].start()
-    labels = []
-    for d in range(1, 16):
-        labels.append(
-            copy(mine, labels_ref.at[s], m_send, m_recv, d, {"seq": lax.rem(s + d, 16)})
-        )
-        labels[-1].start()
-    for one in labels:
+    for one in small:
         one.wait_recv()
 
     feature = iota((HD, 1), 0)
@@ -179,8 +255,6 @@
     w_ring[5].start()
     t_ring[2].wait_recv()
     t_ring[3].wait_recv()
-    w_ring[2].wait_recv()
-    w_ring[3].wait_recv()
 
     def turn(part, k):
         cosine, ahead, behind = tables[k]
@@ -198,40 +272,31 @@
             axis=0,
         ).astype(BF16)
 
-    up, down, far = lax.rem(b + 1, 4), lax.rem(b + 3, 4), lax.rem(b + 2, 4)
-    sends = {}
-
-    def send_to(k, head, n, where, slot):
-        prod[slot] = block(k, head)
-        sends[n] = copy(prod.at[slot], out_ref.at[b, pairs[k]], p_send, p_recv, n, where)
+    sends = []
+
+    def send_to(k, off):
+        n = len(sends)
+        prod[n] = block(k, lax.rem(b + off, 4))
+        sends.append(remote(prod.at[n], out_ref.at[b, pairs[k]], p_send, p_recv, n, on_b(off)))
         sends[n].start()
 
-    def send_far(k, n, where, slot):
-        prod[slot] = block(k, far)
-        sends[n] = copy(prod.at[slot], relay.at[k], p_send, p_recv, n, where)
-        sends[n].start()
-
-    send_to(0, up, 0, on_b(1), 0)
-    send_to(0, down, 2, on_b(3), 1)
+    out_ref[b, pairs[0]] = block(0, b)
+    w_ring[2].wait_recv()
+    w_ring[3].wait_recv()
+    send_to(0, 1)
+    send_to(0, 3)
+    t_ring[4].wait_recv()
+    t_ring[5].wait_recv()
+    send_to(1, 1)
+    send_to(1, 3)
     w_ring[4].wait_recv()
     w_ring[5].wait_recv()
-    send_far(0, 4, on_b(1), 2)
-    t_ring[4].wait_recv()
-    t_ring[5].wait_recv()
-    send_far(1, 5, on_b(3), 3)
-    send_to(1, up, 1, on_b(1), 4)
-    send_to(1, down, 3, on_b(3), 5)
-    out_ref[b, pairs[0]] = block(0, b)
-    sends[4].wait_recv()
-    sends[6] = copy(relay.at[0], out_ref.at[down, pairs[0]], p_send, p_recv, 6, on_b(1))
-    sends[6].start()
-    sends[5].wait_recv()
-    sends[7] = copy(relay.at[1], out_ref.at[up, pairs[1]], p_send, p_recv, 7, on_b(3))
-    sends[7].start()
+    send_to(0, 2)
+    send_to(1, 2)
     out_ref[b, pairs[1]] = block(1, b)
-    for n in (0, 1, 2, 3, 6, 7):
-        sends[n].wait_recv()
-    for one in w_ring + t_ring + labels + list(sends.values()):
+    for one in sends:
+        one.wait_recv()
+    for one in w_ring + t_ring + small + sends:
         one.wait_send()
 
 
@@ -319,7 +384,8 @@
         _, denominator, acc = lax.fori_loop(
             begin // wide, (end + wide - 1) // wide, one_step, state
         )
-        out_ref[s] = (acc / denominator).astype(BF16)
+        out_ref[s, :, :HD] = (acc / denominator).astype(BF16)
+        out_ref[s, :, HD:] = jnp.zeros((ROWS, 128 - HD), BF16)
         return carry
 
     lax.fori_loop(0, 16, one_block, 0)
@@ -342,21 +408,22 @@
     acc,
     tiles,
     mg,
+    wv,
+    l_sem,
     h_send,
     h_recv,
     g_send,
     g_recv,
+    b_send,
+    b_recv,
     z_send,
     z_recv,
     c_send,
     c_recv,
-    b_send,
-    b_recv,
 ):
     s = lax.axis_index("seq")
     p = lax.axis_index("pack")
     nz = n_pack // 2
-    z, core = p // 2, lax.rem(p, 2)
     y, x = s // 4, lax.rem(s, 4)
 
     barrier = pltpu.get_barrier_semaphore()
@@ -368,39 +435,34 @@
         pl.semaphore_signal(
             barrier, inc=1, device_id={"pack": lax.rem(p + d, n_pack)}, device_id_type=MESH
         )
+    load = pltpu.make_async_copy(wm_ref, wv, l_sem)
+    load.start()
+    tables_ref[p] = table_ref[...]
+    rows_ref[p, :, :, OUTC:] = jnp.zeros((4, 4 * GROUPS, 256 - OUTC), BF16)
     pl.semaphore_wait(barrier, 15 + n_pack - 1)
-
-    def copy(src, dst, send, recv, k, where):
-        return pltpu.make_async_remote_copy(
-            src_ref=src,
-            dst_ref=dst,
-            send_sem=send.at[k],
-            recv_sem=recv.at[k],
-            device_id=where,
-            device_id_type=MESH,
-        )
 
     out = []
     back = []
     for d in range(1, 16):
         to = lax.rem(s + d, 16)
-        back.append(copy(att_ref.at[to], heads.at[s], h_send, h_recv, d, {"seq": to}))
+        back.append(remote(att_ref.at[to], heads.at[s], h_send, h_recv, d, {"seq": to}))
         back[-1].start()
     tabs = []
     for d in range(1, n_pack):
         tabs.append(
-            copy(table_ref, tables_ref.at[p], b_send, b_recv, d, {"pack": lax.rem(p + d, n_pack)})
+            remote(table_ref, tables_ref.at[p], b_send, b_recv, d, {"pack": lax.rem(p + d, n_pack)})
         )
         tabs[-1].start()
-    tables_ref[p] = table_ref[...]
     out += back + tabs
     inputs = embedded(patches_ref, mask_ref, embed_ref)
-    acc[...] = inputs + jnp.dot(att_ref[s], wo_ref[s], preferred_element_type=F32)
+    acc[...] = inputs + jnp.dot(
+        att_ref[s][:, :HD], wo_ref[s], preferred_element_type=F32
+    )
     for d in range(1, 16):
         back[d - 1].wait_recv()
         head = lax.rem(s + 16 - d, 16)
-        acc[...] += jnp.dot(heads[head], wo_ref[head], preferred_element_type=F32)
-    normed = layer_norm(acc[...], gain_ref[...].astype(F32))
+        acc[...] += jnp.dot(heads[head][:, :HD], wo_ref[head], preferred_element_type=F32)
+    normed = layer_norm(acc[...], gain_ref[...].astype(F32).reshape(1, D))
     for t in range(D // 128):
         tiles[t] = normed[:, 128 * t : 128 * (t + 1)]
     for t in range(D // 128):
@@ -426,7 +488,7 @@
             ref = mg.at[blk, pl.ds(2 * half, 2)]
         else:
             ref = mg.at[blk, pl.ds(2 * half + kind - 2, 1)]
-        one = copy(ref, ref, g_send, g_recv, k, {"seq": to})
+        one = remote(ref, ref, g_send, g_recv, k, {"seq": to})
         one.start()
         started[half, phase, order[df] if phase else 0, kind] = one
         out.append(one)
@@ -455,47 +517,38 @@
             done.add((half, df, dg))
             arrive(half, df, dg)
 
-    z_out = {}
-
-    def z_copy(ref, k, step, c):
-        if step == 2:
-            return copy(ref, ref, c_send, c_recv, c * nz + k, {"pack": z * 2 + 1 - core})
-        to = lax.rem(z + step + nz, nz) * 2 + core
-        return copy(ref, ref, z_send, z_recv, (c * 2 + (step + 1) // 2) * nz + k, {"pack": to})
-
-    def chunk(c, dy):
+    z_rings = []
+
+    def launch(row, part):
+        one = PackRing(
+            n_pack,
+            lambda pack: rows_ref.at[pack, row, part],
+            limits_of(nz, len(z_rings)),
+            (z_send, z_recv, c_send, c_recv),
+            len(z_rings),
+        )
+        one.start()
+        z_rings.append(one)
+
+    def chunk(dy, pieces):
         row = lax.rem(y + dy + 4, 4)
-        total = jnp.broadcast_to(bias_ref[...].astype(F32), (4 * GROUPS, OUTC))
+        total = jnp.broadcast_to(
+            bias_ref[...].astype(F32).reshape(1, OUTC), (4 * GROUPS, OUTC)
+        )
         for j in range(4):
             part = mg[pl.ds(4 * row, 4), j].reshape(4 * GROUPS, D)
             total += lax.dot_general(
-                part, wm_ref[:, pl.ds(j * D, D)], NT, preferred_element_type=F32
+                part, wv[:, pl.ds(j * D, D)], NT, preferred_element_type=F32
             )
-        rows_ref[p, row] = total.astype(BF16)
-        own = rows_ref.at[p, row]
-        for step in (1, -1, 2):
-            z_out[c, step, 0] = z_copy(own, 0, step, c)
-            z_out[c, step, 0].start()
-
-    def hops(c):
-        return (nz // 2, nz - 1 - nz // 2) if c % 2 == 0 else (nz - 1 - nz // 2, nz // 2)
-
-    def pass_on(c, dy):
-        row = lax.rem(y + dy + 4, 4)
-        limits = hops(c)
-        for h in range(1, max(limits) + 1):
-            for step, limit in ((1, limits[0]), (-1, limits[1])):
-                if h > limit:
-                    continue
-                z_out[c, step, h - 1].wait_recv()
-                pack = lax.rem(z - step * h + nz, nz) * 2 + core
-                ref = rows_ref.at[pack, row]
-                if h < limit:
-                    z_out[c, step, h] = z_copy(ref, h, step, c)
-                    z_out[c, step, h].start()
-                k = h if step == 1 else limits[0] + h
-                z_out[c, 2, k] = z_copy(ref, k, 2, c)
-                z_out[c, 2, k].start()
+        rows_ref[p, row, :, :OUTC] = total.astype(BF16)
+        size = 4 * GROUPS // pieces
+        for n in range(pieces):
+            launch(row, pl.ds(n * size, size))
+
+    def hop(*which):
+        for c, h in which:
+            if h <= nz // 2:
+                z_rings[c].hop(h)
 
     for half in range(2):
         send(half, 0, 0, 0, 0)
@@ -518,27 +571,30 @@
             need(1, dy, dx)
 
     row_ready(0)
-    chunk(0, 0)
+    load.wait()
+    chunk(0, 1)
     for df in (-1, 1, 2):
         for dg in (-1, 1):
             for half in range(2):
                 need(half, df, dg)
+    hop((0, 1))
     row_ready(-1)
-    chunk(1, -1)
-    pass_on(0, 0)
+    chunk(-1, 1)
+    hop((0, 2))
     row_ready(1)
-    chunk(2, 1)
-    pass_on(1, -1)
+    chunk(1, 1)
+    hop((0, 3), (1, 1), (2, 1), (0, 4), (1, 2), (2, 2), (1, 3), (2, 3))
     row_ready(2)
-    chunk(3, 2)
-    pass_on(2, 1)
-    pass_on(3, 2)
-    for c in range(4):
-        for k in range(nz):
-            z_out[c, 2, k].wait_recv()
+    chunk(2, 2)
+    hop((1, 4), (2, 4))
+    for h in range(1, nz // 2 + 1):
+        hop((3, h), (4, h))
+    for one in z_rings:
+        one.finish()
+        one.drain()
     for one in tabs:
         one.wait_recv()
-    for one in out + list(z_out.values()):
+    for one in out:
         one.wait_send()
 
 
@@ -556,7 +612,7 @@
         pick = ((source == slot + (first - base)) & (slot < length)).astype(BF16)
         out_ref[0, q] = jnp.dot(
             pick, rows_ref[q, pl.ds(base, window)], preferred_element_type=F32
-        ).astype(BF16)
+        )[:, :OUTC].astype(BF16)
 
 
 def local(
@@ -578,24 +634,27 @@
     nz = n_pack // 2
     dma = pltpu.SemaphoreType.DMA
     shape = jax.ShapeDtypeStruct
-    embed = mask_embed[None, :]
+    embed = mask_embed
+    wm = merge_weight.T
     qkv, labels = pl.pallas_call(
         qkv_kernel,
-        out_shape=(shape((4, 2, 3 * HD, 2 * ROWS), BF16), shape((16, 8, ROWS), jnp.int32)),
+        out_shape=(
+            shape((4, 2, 3 * HD, 2 * ROWS), BF16),
+            shape((16, 8, ROWS), jnp.int32),
+        ),
         in_specs=[VM] * 8,
         out_specs=(VM, VM),
         scratch_shapes=[
             pltpu.VMEM((4, ROWS, D), BF16),
             pltpu.VMEM((4, 3 * HD, D), BF16),
             pltpu.VMEM((6, 3 * HD, 2 * ROWS), BF16),
-            pltpu.VMEM((2, 3 * HD, 2 * ROWS), BF16),
             pltpu.VMEM((8, ROWS), jnp.int32),
             dma((6,)),
             dma((6,)),
             dma((6,)),
             dma((6,)),
-            dma((8,)),
-            dma((8,)),
+            dma((6,)),
+            dma((6,)),
             dma((16,)),
             dma((16,)),
         ],
@@ -607,7 +666,7 @@
         patches,
         patch_mask,
         embed,
-        norm_gain[None, :],
+        norm_gain,
         qkv_weight.T,
         segment_ids,
         patch_rows,
@@ -615,7 +674,7 @@
     )
     attended, table = pl.pallas_call(
         functools.partial(attention_kernel, n_pack),
-        out_shape=(shape((16, ROWS, HD), BF16), shape((8, 128), jnp.int32)),
+        out_shape=(shape((16, ROWS, 128), BF16), shape((8, 128), jnp.int32)),
         in_specs=[VM, VM, SM],
         out_specs=(VM, VM),
         scratch_shapes=[
@@ -629,26 +688,28 @@
     rows, tables = pl.pallas_call(
         functools.partial(merge_kernel, n_pack),
         out_shape=(
-            shape((n_pack, 4, 4 * GROUPS, OUTC), BF16),
+            shape((n_pack, 4, 4 * GROUPS, 256), BF16),
             shape((n_pack, 8, 128), jnp.int32),
         ),
-        in_specs=[VM] * 9,
+        in_specs=[VM] * 6 + [ANY, VM, VM],
         out_specs=(VM, VM),
         scratch_shapes=[
-            pltpu.VMEM((16, ROWS, HD), BF16),
+            pltpu.VMEM((16, ROWS, 128), BF16),
             pltpu.VMEM((ROWS, D), F32),
             pltpu.VMEM((D // 128, ROWS, 128), F32),
             pltpu.VMEM((16, 4, GROUPS, D), BF16),
+            pltpu.VMEM((OUTC, 4 * D), BF16),
+            dma,
             dma((16,)),
             dma((16,)),
             dma((64,)),
             dma((64,)),
-            dma((8 * nz,)),
-            dma((8 * nz,)),
-            dma((4 * nz,)),
-            dma((4 * nz,)),
             dma((n_pack,)),
             dma((n_pack,)),
+            dma((10 * nz,)),
+            dma((10 * nz,)),
+            dma((5 * nz,)),
+            dma((5 * nz,)),
         ],
         compiler_params=pltpu.CompilerParams(
             collective_id=1, has_side_effects=True, vmem_limit_bytes=60 * 2**20
@@ -660,9 +721,9 @@
         patch_mask,
         embed,
         out_weight.reshape(HEADS, HD, D),
-        merge_gain[None, :],
-        merge_weight.T,
-        merge_bias[None, :],
+        merge_gain,
+        wm,
+        merge_bias,
         table,
     )
     return pl.pallas_call(
@@ -672,7 +733,7 @@
         out_specs=VM,
         compiler_params=pltpu.CompilerParams(vmem_limit_bytes=60 * 2**20),
         name="select",
-    )(rows.reshape(n_pack, 4 * MOST, OUTC), tables)
+    )(rows.reshape(n_pack, 4 * MOST, 256), tables)
 
 
 def solution(mesh):

time: 214 us -> 182 us (0.85)
  Pallas kernels: 209 us -> 182 us
  local copies, waits for them, and re-layouts: 5.02 us -> 0 us
    pallas_call x1, Pallas kernels: 132 us -> 110 us  [local(): pl.pallas_call(functools.partial(merge_kernel, n_pack), out_shape=(shape(...]
    broadcast_in_dim x4 -> x0, local copies, waits for them, and re-layouts: 5.02 us -> none  [the longest x1 1.28 us: local(): norm_gain[None, :]]
    pallas_call x1, Pallas kernels: 47.2 us -> 42.4 us  [local(): pl.pallas_call(qkv_kernel, out_shape=(shape((4, 2, 3 * HD, 2 * ROWS), BF1...]
where the time goes in v2:
time: 182 us
  Pallas kernels  182 us (100%)
    pallas_call x1, Pallas kernels, local(): pl.pallas_call(functools.partial(merge_kernel, n_pack), out_shape=(shape(...  110 us
    pallas_call x1, Pallas kernels, local(): pl.pallas_call(qkv_kernel, out_shape=(shape((4, 2, 3 * HD, 2 * ROWS), BF1...  42.4 us
    pallas_call x1, Pallas kernels, local(): pl.pallas_call(functools.partial(attention_kernel, n_pack), out_shape=(sh...  24.8 us
    pallas_call x1, Pallas kernels, local(): pl.pallas_call(functools.partial(select_kernel, n_pack), out_shape=shape(...  4.83 us

profile of v2, /device:TPU:1, one launch (start us, length us, event | category | flops | bytes accessed | tf_op | source)
XLA Modules:
  0.0 182.4 jit_solution(11646813179107437967)
XLA Ops:
  0.0 42.4 %qkv.1 = (bf16[4,2,264,384]{3,2,1,0:T(8,128)(2,1)}, s32[16,8,192]{2,1,0:T(8,128)}) custom-call(bf16[1,192,1408]{2,1,0:T(8,128)(2,1)} %patches_ref.3, s32[1,192]{1,0:T(1,128)} %mask_ref.3, bf16[1408]{0:T(1024)(128)(2,1)} %embed_ref.3, bf16[1408]{0:T(1024)(128)(2,1)} %gain_ref.2, bf16[264,1408]{1,0:T(8,128)(2,1)} %bitcast.7, s32[1,192]{1,0:T(1,128)} %seg_ref.1, ...), custom_call_target="tpu_custom_call" | custom-call | tf_op jit(solution)/shard_map/qkv/pallas_call | solution.py:639
  42.5 24.8 %attention.1 = (bf16[16,192,128]{2,1,0:T(8,128)(2,1)}, s32[8,128]{1,0:T(8,128)}) custom-call(bf16[4,2,264,384]{3,2,1,0:T(8,128)(2,1)} %get-tuple-element.11.qkv_ref, s32[16,8,192]{2,1,0:T(8,128)} %get-tuple-element.12.labels_ref, s32[1,8]{1,0:T(1,128)} %owner_ref.1), custom_call_target="tpu_custom_call" | custom-call | tf_op jit(solution)/shard_map/attention/pallas_call | solution.py:675
  67.3 110.3 %merge.1 = (bf16[16,4,192,256]{3,2,1,0:T(8,128)(2,1)}, s32[16,8,128]{2,1,0:T(8,128)}) custom-call(bf16[16,192,128]{2,1,0:T(8,128)(2,1)} %get-tuple-element.13.att_ref, bf16[1,192,1408]{2,1,0:T(8,128)(2,1)} %patches_ref.3, s32[1,192]{1,0:T(1,128)} %mask_ref.3, bf16[1408]{0:T(1024)(128)(2,1)} %embed_ref.3, bf16[16,88,1408]{2,1,0:T(8,128)(2,1)} %bitcast.5, ...), custom_call_target="tpu_custom_call" | custom-call | tf_op jit(solution)/shard_map/merge/pallas_call | solution.py:688
  177.6 4.8 %select.1 = bf16[1,16,192,224]{3,2,1,0:T(8,128)(2,1)} custom-call(bf16[16,768,256]{2,1,0:T(8,128)(2,1)} %bitcast.4, s32[16,8,128]{2,1,0:T(8,128)} %get-tuple-element.16.tables_ref), custom_call_target="tpu_custom_call" | custom-call | tf_op jit(solution)/shard_map/select/pallas_call | solution.py:729

commit v3 on v2

--- a/solution.py
+++ b/solution.py
@@ -131,6 +131,14 @@
     def drain(self):
         for one in self.made.values():
             one.wait_send()
+
+
+ORDER = (
+    (0, 0), (-1, 0), (1, 0), (0, -1), (0, 1),
+    (2, 0), (0, 2),
+    (-1, -1), (1, -1), (-1, 1), (1, 1),
+    (2, -1), (2, 1), (-1, 2), (1, 2), (2, 2),
+)
 
 
 def limits_of(nz, c):
@@ -300,7 +308,7 @@
         one.wait_send()
 
 
-def attention_kernel(n_pack, qkv_ref, labels_ref, owner_ref, out_ref, table_ref, qs, kvs, segs):
+def attention_kernel(n_pack, qkv_ref, labels_ref, owner_ref, out_ref, table_ref, kvs, segs, keys, marks, values):
     core = lax.rem(lax.axis_index("pack"), 2)
     half = ROWS
     wide = 2 * ROWS
@@ -324,14 +332,14 @@
             kvs[m] = jnp.where(lane < half, left, right).astype(BF16)
 
     for m in range(8):
-        turned = jnp.concatenate(
-            [kvs[m].astype(F32)[:HD], jnp.zeros((128 - HD, wide), F32)], axis=0
-        ).T
-        qs[2 * m] = turned[:half].astype(BF16)
-        qs[2 * m + 1] = turned[half:].astype(BF16)
         segs[m] = side_by_side(
             labels_ref[2 * m].astype(F32), labels_ref[2 * m + 1].astype(F32)
         )
+        fill = jnp.zeros((128 - HD, wide), F32)
+        both = kvs[m].astype(F32)
+        keys[m] = jnp.concatenate([both[HD : 2 * HD], fill], axis=0).T.astype(BF16)
+        values[m] = jnp.concatenate([both[2 * HD :], fill], axis=0).astype(BF16)
+        marks[m] = column_of(segs[m][0:1])
 
     every = jnp.concatenate([labels_ref[k][0:1] for k in range(16)], axis=0)
     total = 16 * ROWS
@@ -353,42 +361,47 @@
     scale = HD ** (-0.5) * 1.4426950408889634
     low = -0.7 * 3.4028235e38
 
-    def one_block(s, carry):
+    size = 2 * wide
+
+    def one_block(g, carry):
         begin = jnp.int32(0)
         end = jnp.int32(total)
         for image in range(1, 8):
-            begin = jnp.where(starts[image] <= s * ROWS, starts[image], begin)
+            begin = jnp.where(starts[image] <= g * size, starts[image], begin)
         for image in range(7, 0, -1):
-            end = jnp.where(starts[image] >= (s + 1) * ROWS, starts[image], end)
-        queries = qs[s][:, :HD]
-        own = column_of(labels_ref[s][0:1].astype(F32))
+            end = jnp.where(starts[image] >= (g + 1) * size, starts[image], end)
+        queries = jnp.concatenate(
+            [kvs[2 * g, pl.ds(0, HD)], kvs[2 * g + 1, pl.ds(0, HD)]], axis=1
+        )
+        own = jnp.concatenate([segs[2 * g][0:1], segs[2 * g + 1][0:1]], axis=1)
 
         def one_step(m, state):
             top, denominator, acc = state
-            scores = jnp.dot(queries, kvs[m, pl.ds(HD, HD)], preferred_element_type=F32)
-            scores = jnp.where(own == segs[m][0:1], scores, low)
-            new_top = jnp.maximum(top, jnp.max(scores, axis=-1, keepdims=True))
+            scores = jnp.dot(keys[m][:, :HD], queries, preferred_element_type=F32)
+            scores = jnp.where(marks[m] == own, scores, low)
+            new_top = jnp.maximum(top, jnp.max(scores, axis=0, keepdims=True))
             shrink = jnp.exp2((top - new_top) * scale)
             weights = jnp.exp2((scores - new_top) * scale)
-            denominator = denominator * shrink + jnp.sum(weights, axis=-1, keepdims=True)
-            acc = acc * shrink + lax.dot_general(
-                weights.astype(BF16), kvs[m, pl.ds(2 * HD, HD)], NT, preferred_element_type=F32
+            denominator = denominator * shrink + jnp.sum(weights, axis=0, keepdims=True)
+            acc = acc * shrink + jnp.dot(
+                values[m], weights.astype(BF16), preferred_element_type=F32
             )
             return new_top, denominator, acc
 
         state = (
-            jnp.full((ROWS, 1), low, F32),
-            jnp.zeros((ROWS, 1), F32),
-            jnp.zeros((ROWS, HD), F32),
+            jnp.full((1, size), low, F32),
+            jnp.zeros((1, size), F32),
+            jnp.zeros((128, size), F32),
         )
         _, denominator, acc = lax.fori_loop(
             begin // wide, (end + wide - 1) // wide, one_step, state
         )
-        out_ref[s, :, :HD] = (acc / denominator).astype(BF16)
-        out_ref[s, :, HD:] = jnp.zeros((ROWS, 128 - HD), BF16)
+        result = (acc / denominator).T
+        for n in range(4):
+            out_ref[4 * g + n] = result[n * ROWS : (n + 1) * ROWS].astype(BF16)
         return carry
 
-    lax.fori_loop(0, 16, one_block, 0)
+    lax.fori_loop(0, total // size, one_block, 0)
 
 
 def merge_kernel(
@@ -438,7 +451,7 @@
     load = pltpu.make_async_copy(wm_ref, wv, l_sem)
     load.start()
     tables_ref[p] = table_ref[...]
-    rows_ref[p, :, :, OUTC:] = jnp.zeros((4, 4 * GROUPS, 256 - OUTC), BF16)
+    rows_ref[p, :, :, OUTC:] = jnp.zeros((16, GROUPS, 256 - OUTC), BF16)
     pl.semaphore_wait(barrier, 15 + n_pack - 1)
 
     out = []
@@ -519,10 +532,10 @@
 
     z_rings = []
 
-    def launch(row, part):
+    def launch(first, count):
         one = PackRing(
             n_pack,
-            lambda pack: rows_ref.at[pack, row, part],
+            lambda pack: rows_ref.at[pack, pl.ds(first, count)],
             limits_of(nz, len(z_rings)),
             (z_send, z_recv, c_send, c_recv),
             len(z_rings),
@@ -530,20 +543,25 @@
         one.start()
         z_rings.append(one)
 
-    def chunk(dy, pieces):
-        row = lax.rem(y + dy + 4, 4)
+    def chunk(first, count, pieces):
+        blocks = ORDER[first : first + count]
         total = jnp.broadcast_to(
-            bias_ref[...].astype(F32).reshape(1, OUTC), (4 * GROUPS, OUTC)
-        )
+            bias_ref[...].astype(F32).reshape(1, OUTC), (count * GROUPS, OUTC)
+        )
+        for dx, dy in blocks:
+            need(0, dx, dy)
+            need(1, dy, dx)
         for j in range(4):
-            part = mg[pl.ds(4 * row, 4), j].reshape(4 * GROUPS, D)
+            part = jnp.concatenate([mg[device(0, dx, dy), j] for dx, dy in blocks], axis=0)
             total += lax.dot_general(
                 part, wv[:, pl.ds(j * D, D)], NT, preferred_element_type=F32
             )
-        rows_ref[p, row, :, :OUTC] = total.astype(BF16)
-        size = 4 * GROUPS // pieces
-        for n in range(pieces):
-            launch(row, pl.ds(n * size, size))
+        total = total.astype(BF16)
+        for n in range(count):
+            rows_ref[p, first + n, :, :OUTC] = total[n * GROUPS : (n + 1) * GROUPS]
+        for n in pieces:
+            launch(first, n)
+            first += n
 
     def hop(*which):
         for c, h in which:
@@ -562,32 +580,25 @@
     for half in range(2):
         need(half, 0, -1)
         need(half, 0, 1)
+    load.wait()
+    chunk(0, 5, (5,))
     for half in range(2):
         need(half, 2, 0)
-
-    def row_ready(dy):
-        for dx in (0, -1, 1, 2):
-            need(0, dx, dy)
-            need(1, dy, dx)
-
-    row_ready(0)
-    load.wait()
-    chunk(0, 1)
-    for df in (-1, 1, 2):
-        for dg in (-1, 1):
-            for half in range(2):
-                need(half, df, dg)
+    chunk(5, 2, (2,))
     hop((0, 1))
-    row_ready(-1)
-    chunk(-1, 1)
-    hop((0, 2))
-    row_ready(1)
-    chunk(1, 1)
-    hop((0, 3), (1, 1), (2, 1), (0, 4), (1, 2), (2, 2), (1, 3), (2, 3))
-    row_ready(2)
-    chunk(2, 2)
-    hop((1, 4), (2, 4))
-    for h in range(1, nz // 2 + 1):
+    for df in (-1, 1):
+        for half in range(2):
+            need(half, df, -1)
+            need(half, df, 1)
+        hop((0, 2), (1, 1)) if df == -1 else hop((0, 3), (1, 2))
+    chunk(7, 4, (4,))
+    for half in range(2):
+        need(half, 2, -1)
+        need(half, 2, 1)
+    hop((0, 4), (1, 3), (1, 4), (2, 1), (2, 2))
+    chunk(11, 5, (3, 2))
+    hop((2, 3), (3, 1), (4, 1), (2, 4))
+    for h in range(2, nz // 2 + 1):
         hop((3, h), (4, h))
     for one in z_rings:
         one.finish()
@@ -598,8 +609,22 @@
         one.wait_send()
 
 
-def select_kernel(n_pack, rows_ref, tables_ref, out_ref):
+def select_kernel(n_pack, arrived_ref, tables_ref, out_ref, rows, sems):
     p = lax.axis_index("pack")
+    s = lax.axis_index("seq")
+    y, x = s // 4, lax.rem(s, 4)
+    loads = []
+    for n, (dx, dy) in enumerate(ORDER):
+        place = lax.rem(y + dy + 4, 4) * 4 + lax.rem(x + dx + 4, 4)
+        start = pl.multiple_of(place * GROUPS, GROUPS)
+        loads.append(
+            pltpu.make_async_copy(
+                arrived_ref.at[:, n], rows.at[:, pl.ds(start, GROUPS)], sems.at[n]
+            )
+        )
+        loads[-1].start()
+    for one in loads:
+        one.wait()
     total = 4 * MOST
     window = MOST + 16
     for q in range(n_pack):
@@ -611,7 +636,7 @@
         source = iota((MOST, window), 1)
         pick = ((source == slot + (first - base)) & (slot < length)).astype(BF16)
         out_ref[0, q] = jnp.dot(
-            pick, rows_ref[q, pl.ds(base, window)], preferred_element_type=F32
+            pick, rows[q, pl.ds(base, window)], preferred_element_type=F32
         )[:, :OUTC].astype(BF16)
 
 
@@ -678,9 +703,11 @@
         in_specs=[VM, VM, SM],
         out_specs=(VM, VM),
         scratch_shapes=[
-            pltpu.VMEM((16, ROWS, 128), BF16),
             pltpu.VMEM((8, 3 * HD, 2 * ROWS), BF16),
             pltpu.VMEM((8, 8, 2 * ROWS), F32),
+            pltpu.VMEM((8, 2 * ROWS, 128), BF16),
+            pltpu.VMEM((8, 2 * ROWS, 1), F32),
+            pltpu.VMEM((8, 128, 2 * ROWS), BF16),
         ],
         compiler_params=pltpu.CompilerParams(vmem_limit_bytes=60 * 2**20),
         name="attention",
@@ -688,7 +715,7 @@
     rows, tables = pl.pallas_call(
         functools.partial(merge_kernel, n_pack),
         out_shape=(
-            shape((n_pack, 4, 4 * GROUPS, 256), BF16),
+            shape((n_pack, 16, GROUPS, 256), BF16),
             shape((n_pack, 8, 128), jnp.int32),
         ),
         in_specs=[VM] * 6 + [ANY, VM, VM],
@@ -729,11 +756,12 @@
     return pl.pallas_call(
         functools.partial(select_kernel, n_pack),
         out_shape=shape((1, n_pack, MOST, OUTC), BF16),
-        in_specs=[VM, VM],
+        in_specs=[ANY, VM],
         out_specs=VM,
+        scratch_shapes=[pltpu.VMEM((n_pack, 4 * MOST, 256), BF16), dma((16,))],
         compiler_params=pltpu.CompilerParams(vmem_limit_bytes=60 * 2**20),
         name="select",
-    )(rows.reshape(n_pack, 4 * MOST, 256), tables)
+    )(rows, tables)
 
 
 def solution(mesh):

time: 182 us -> 173 us (0.951)
  Pallas kernels: 182 us -> 172 us
    pallas_call x1, Pallas kernels: 24.8 us -> 17.8 us  [local(): pl.pallas_call(functools.partial(attention_kernel, n_pack), out_shape=(sh...]
    pallas_call x1, Pallas kernels: 110 us -> 106 us  [local(): pl.pallas_call(functools.partial(merge_kernel, n_pack), out_shape=(shape(...]
where the time goes in v3:
time: 173 us; the launch traced here: 172 us
  Pallas kernels  172 us (99%)
    pallas_call x1, Pallas kernels, local(): pl.pallas_call(functools.partial(merge_kernel, n_pack), out_shape=(shape(...  106 us
    pallas_call x1, Pallas kernels, local(): pl.pallas_call(qkv_kernel, out_shape=(shape((4, 2, 3 * HD, 2 * ROWS), BF1...  42.4 us
    pallas_call x1, Pallas kernels, local(): pl.pallas_call(functools.partial(attention_kernel, n_pack), out_shape=(sh...  17.8 us
    pallas_call x1, Pallas kernels, local(): pl.pallas_call(functools.partial(select_kernel, n_pack), out_shape=shape(...  5.79 us

profile of v3, /device:TPU:1, one launch (start us, length us, event | category | flops | bytes accessed | tf_op | source)
XLA Modules:
  0.0 172.2 jit_solution(15420001546095225275)
XLA Ops:
  0.0 42.4 %qkv.1 = (bf16[4,2,264,384]{3,2,1,0:T(8,128)(2,1)}, s32[16,8,192]{2,1,0:T(8,128)}) custom-call(bf16[1,192,1408]{2,1,0:T(8,128)(2,1)} %patches_ref.3, s32[1,192]{1,0:T(1,128)} %mask_ref.3, bf16[1408]{0:T(1024)(128)(2,1)} %embed_ref.3, bf16[1408]{0:T(1024)(128)(2,1)} %gain_ref.2, bf16[264,1408]{1,0:T(8,128)(2,1)} %bitcast.5, s32[1,192]{1,0:T(1,128)} %seg_ref.1, ...), custom_call_target="tpu_custom_call" | custom-call | tf_op jit(solution)/shard_map/qkv/pallas_call | solution.py:664
  42.5 17.8 %attention.1 = (bf16[16,192,128]{2,1,0:T(8,128)(2,1)}, s32[8,128]{1,0:T(8,128)}) custom-call(bf16[4,2,264,384]{3,2,1,0:T(8,128)(2,1)} %get-tuple-element.11.qkv_ref, s32[16,8,192]{2,1,0:T(8,128)} %get-tuple-element.12.labels_ref, s32[1,8]{1,0:T(1,128)} %owner_ref.1), custom_call_target="tpu_custom_call" | custom-call | tf_op jit(solution)/shard_map/attention/pallas_call | solution.py:700
  60.3 105.9 %merge.1 = (bf16[16,16,48,256]{3,2,1,0:T(8,128)(2,1)}, s32[16,8,128]{2,1,0:T(8,128)}) custom-call(bf16[16,192,128]{2,1,0:T(8,128)(2,1)} %get-tuple-element.13.att_ref, bf16[1,192,1408]{2,1,0:T(8,128)(2,1)} %patches_ref.3, s32[1,192]{1,0:T(1,128)} %mask_ref.3, bf16[1408]{0:T(1024)(128)(2,1)} %embed_ref.3, bf16[16,88,1408]{2,1,0:T(8,128)(2,1)} %bitcast.3, ...), custom_call_target="tpu_custom_call" | custom-call | tf_op jit(solution)/shard_map/merge/pallas_call | solution.py:715
  166.2 5.8 %select.1 = bf16[1,16,192,224]{3,2,1,0:T(8,128)(2,1)} custom-call(bf16[16,16,48,256]{3,2,1,0:T(8,128)(2,1)} %get-tuple-element.15.arrived_ref, s32[16,8,128]{2,1,0:T(8,128)} %get-tuple-element.16.tables_ref), custom_call_target="tpu_custom_call" | custom-call | tf_op jit(solution)/shard_map/select/pallas_call | solution.py:756

commit v4 on v3

--- a/solution.py
+++ b/solution.py
@@ -131,6 +131,24 @@
     def drain(self):
         for one in self.made.values():
             one.wait_send()
+
+
+class PackDirect(PackRing):
+    def start(self):
+        z_send, z_recv, c_send, c_recv = self.sems
+        ref = self.ref_of(self.p)
+        self.go(self.p, 2, 0)
+        steps = [k for n in range(1, self.nz // 2 + 1) for k in (n, self.nz - n)]
+        for k in dict.fromkeys(steps):
+            to = lax.rem(self.z + k, self.nz) * 2 + self.core
+            one = remote(ref, ref, z_send, z_recv, self.base * 2 * self.nz + k, {"pack": to})
+            one.start()
+            self.made[1, k] = one
+
+    def share(self):
+        for k in range(1, self.nz):
+            self.made[1, k].wait_recv()
+            self.go(lax.rem(self.z - k + self.nz, self.nz) * 2 + self.core, 2, k)
 
 
 ORDER = (
@@ -532,8 +550,8 @@
 
     z_rings = []
 
-    def launch(first, count):
-        one = PackRing(
+    def launch(first, count, kind):
+        one = kind(
             n_pack,
             lambda pack: rows_ref.at[pack, pl.ds(first, count)],
             limits_of(nz, len(z_rings)),
@@ -543,7 +561,7 @@
         one.start()
         z_rings.append(one)
 
-    def chunk(first, count, pieces):
+    def chunk(first, count, pieces, kind=PackRing):
         blocks = ORDER[first : first + count]
         total = jnp.broadcast_to(
             bias_ref[...].astype(F32).reshape(1, OUTC), (count * GROUPS, OUTC)
@@ -560,7 +578,7 @@
         for n in range(count):
             rows_ref[p, first + n, :, :OUTC] = total[n * GROUPS : (n + 1) * GROUPS]
         for n in pieces:
-            launch(first, n)
+            launch(first, n, kind)
             first += n
 
     def hop(*which):
@@ -581,25 +599,24 @@
         need(half, 0, -1)
         need(half, 0, 1)
     load.wait()
-    chunk(0, 5, (5,))
+    chunk(0, 5, (5,), PackDirect)
     for half in range(2):
         need(half, 2, 0)
-    chunk(5, 2, (2,))
-    hop((0, 1))
+    chunk(5, 2, (2,), PackDirect)
     for df in (-1, 1):
         for half in range(2):
             need(half, df, -1)
             need(half, df, 1)
-        hop((0, 2), (1, 1)) if df == -1 else hop((0, 3), (1, 2))
     chunk(7, 4, (4,))
     for half in range(2):
         need(half, 2, -1)
         need(half, 2, 1)
-    hop((0, 4), (1, 3), (1, 4), (2, 1), (2, 2))
     chunk(11, 5, (3, 2))
-    hop((2, 3), (3, 1), (4, 1), (2, 4))
+    hop((2, 1), (3, 1), (4, 1))
+    z_rings[0].share()
+    z_rings[1].share()
     for h in range(2, nz // 2 + 1):
-        hop((3, h), (4, h))
+        hop((2, h), (3, h), (4, h))
     for one in z_rings:
         one.finish()
         one.drain()

time: 173 us -> 161 us (0.931)
  Pallas kernels: 172 us -> 161 us
    pallas_call x1, Pallas kernels: 106 us -> 98.1 us  [local(): pl.pallas_call(functools.partial(merge_kernel, n_pack), out_shape=(shape(...]
    pallas_call x1, Pallas kernels: 17.8 us -> 14.9 us  [local(): pl.pallas_call(functools.partial(attention_kernel, n_pack), out_shape=(sh...]
where the time goes in v4:
time: 161 us
  Pallas kernels  161 us (100%)
    pallas_call x1, Pallas kernels, local(): pl.pallas_call(functools.partial(merge_kernel, n_pack), out_shape=(shape(...  98.1 us
    pallas_call x1, Pallas kernels, local(): pl.pallas_call(qkv_kernel, out_shape=(shape((4, 2, 3 * HD, 2 * ROWS), BF1...  42.4 us
    pallas_call x1, Pallas kernels, local(): pl.pallas_call(functools.partial(attention_kernel, n_pack), out_shape=(sh...  14.9 us
    pallas_call x1, Pallas kernels, local(): pl.pallas_call(functools.partial(select_kernel, n_pack), out_shape=shape(...  5.8 us

profile of v4, /device:TPU:1, one launch (start us, length us, event | category | flops | bytes accessed | tf_op | source)
XLA Modules:
  0.0 161.4 jit_solution(15665083412833470872)
XLA Ops:
  0.0 42.4 %qkv.1 = (bf16[4,2,264,384]{3,2,1,0:T(8,128)(2,1)}, s32[16,8,192]{2,1,0:T(8,128)}) custom-call(bf16[1,192,1408]{2,1,0:T(8,128)(2,1)} %patches_ref.3, s32[1,192]{1,0:T(1,128)} %mask_ref.3, bf16[1408]{0:T(1024)(128)(2,1)} %embed_ref.3, bf16[1408]{0:T(1024)(128)(2,1)} %gain_ref.2, bf16[264,1408]{1,0:T(8,128)(2,1)} %bitcast.5, s32[1,192]{1,0:T(1,128)} %seg_ref.1, ...), custom_call_target="tpu_custom_call" | custom-call | tf_op jit(solution)/shard_map/qkv/pallas_call | solution.py:681
  42.5 14.9 %attention.1 = (bf16[16,192,128]{2,1,0:T(8,128)(2,1)}, s32[8,128]{1,0:T(8,128)}) custom-call(bf16[4,2,264,384]{3,2,1,0:T(8,128)(2,1)} %get-tuple-element.11.qkv_ref, s32[16,8,192]{2,1,0:T(8,128)} %get-tuple-element.12.labels_ref, s32[1,8]{1,0:T(1,128)} %owner_ref.1), custom_call_target="tpu_custom_call" | custom-call | tf_op jit(solution)/shard_map/attention/pallas_call | solution.py:717
  57.3 98.1 %merge.1 = (bf16[16,16,48,256]{3,2,1,0:T(8,128)(2,1)}, s32[16,8,128]{2,1,0:T(8,128)}) custom-call(bf16[16,192,128]{2,1,0:T(8,128)(2,1)} %get-tuple-element.13.att_ref, bf16[1,192,1408]{2,1,0:T(8,128)(2,1)} %patches_ref.3, s32[1,192]{1,0:T(1,128)} %mask_ref.3, bf16[1408]{0:T(1024)(128)(2,1)} %embed_ref.3, bf16[16,88,1408]{2,1,0:T(8,128)(2,1)} %bitcast.3, ...), custom_call_target="tpu_custom_call" | custom-call | tf_op jit(solution)/shard_map/merge/pallas_call | solution.py:732
  155.5 5.8 %select.1 = bf16[1,16,192,224]{3,2,1,0:T(8,128)(2,1)} custom-call(bf16[16,16,48,256]{3,2,1,0:T(8,128)(2,1)} %get-tuple-element.15.arrived_ref, s32[16,8,128]{2,1,0:T(8,128)} %get-tuple-element.16.tables_ref), custom_call_target="tpu_custom_call" | custom-call | tf_op jit(solution)/shard_map/select/pallas_call | solution.py:773

commit v5 on v4

--- a/solution.py
+++ b/solution.py
@@ -214,6 +214,8 @@
     mine[2:3, :] = col_ref[...]
     mine[3:8, :] = jnp.zeros((5, ROWS), jnp.int32)
     labels_ref[s] = mine[...]
+    inputs = embedded(patches_ref, mask_ref, embed_ref)
+    tok[a] = layer_norm(inputs, gain_ref[...].astype(F32).reshape(1, D)).astype(BF16)
     pl.semaphore_wait(barrier, 15)
 
     w_ring = ring_of_four(
@@ -245,8 +247,6 @@
         one.start()
     w_ring[2].start()
     w_ring[3].start()
-    inputs = embedded(patches_ref, mask_ref, embed_ref)
-    tok[a] = layer_norm(inputs, gain_ref[...].astype(F32).reshape(1, D)).astype(BF16)
     for k in range(4):
         t_ring[k].start()
     wts[b] = weight_ref[...]
@@ -428,7 +428,7 @@
     patches_ref,
     mask_ref,
     embed_ref,
-    wo_ref,
+    wo_hbm,
     gain_ref,
     wm_ref,
     bias_ref,
@@ -440,6 +440,7 @@
     tiles,
     mg,
     wv,
+    wo_ref,
     l_sem,
     h_send,
     h_recv,
@@ -466,7 +467,9 @@
         pl.semaphore_signal(
             barrier, inc=1, device_id={"pack": lax.rem(p + d, n_pack)}, device_id_type=MESH
         )
-    load = pltpu.make_async_copy(wm_ref, wv, l_sem)
+    first_load = pltpu.make_async_copy(wo_hbm, wo_ref, l_sem.at[0])
+    first_load.start()
+    load = pltpu.make_async_copy(wm_ref, wv, l_sem.at[1])
     load.start()
     tables_ref[p] = table_ref[...]
     rows_ref[p, :, :, OUTC:] = jnp.zeros((16, GROUPS, 256 - OUTC), BF16)
@@ -486,6 +489,7 @@
         tabs[-1].start()
     out += back + tabs
     inputs = embedded(patches_ref, mask_ref, embed_ref)
+    first_load.wait()
     acc[...] = inputs + jnp.dot(
         att_ref[s][:, :HD], wo_ref[s], preferred_element_type=F32
     )
@@ -611,12 +615,12 @@
     for half in range(2):
         need(half, 2, -1)
         need(half, 2, 1)
-    chunk(11, 5, (3, 2))
-    hop((2, 1), (3, 1), (4, 1))
+    chunk(11, 5, (2, 2, 1))
+    hop((2, 1), (3, 1), (4, 1), (5, 1))
     z_rings[0].share()
     z_rings[1].share()
     for h in range(2, nz // 2 + 1):
-        hop((2, h), (3, h), (4, h))
+        hop((2, h), (3, h), (4, h), (5, h))
     for one in z_rings:
         one.finish()
         one.drain()
@@ -630,21 +634,27 @@
     p = lax.axis_index("pack")
     s = lax.axis_index("seq")
     y, x = s // 4, lax.rem(s, 4)
+    part = n_pack // 2
     loads = []
-    for n, (dx, dy) in enumerate(ORDER):
-        place = lax.rem(y + dy + 4, 4) * 4 + lax.rem(x + dx + 4, 4)
-        start = pl.multiple_of(place * GROUPS, GROUPS)
-        loads.append(
-            pltpu.make_async_copy(
-                arrived_ref.at[:, n], rows.at[:, pl.ds(start, GROUPS)], sems.at[n]
+    for h in range(2):
+        packs = pl.ds(h * part, part)
+        for n, (dx, dy) in enumerate(ORDER):
+            place = lax.rem(y + dy + 4, 4) * 4 + lax.rem(x + dx + 4, 4)
+            start = pl.multiple_of(place * GROUPS, GROUPS)
+            loads.append(
+                pltpu.make_async_copy(
+                    arrived_ref.at[packs, n],
+                    rows.at[packs, pl.ds(start, GROUPS)],
+                    sems.at[16 * h + n],
+                )
             )
-        )
-        loads[-1].start()
-    for one in loads:
-        one.wait()
+            loads[-1].start()
     total = 4 * MOST
     window = MOST + 16
     for q in range(n_pack):
+        if q % part == 0:
+            for one in loads[16 * (q // part) :][:16]:
+                one.wait()
         mine = iota((1, 128), 1) == p
         first = jnp.sum(jnp.where(mine, tables_ref[q, 0:1, :], 0))
         length = jnp.sum(jnp.where(mine, tables_ref[q, 1:2, :], 0))
@@ -735,7 +745,7 @@
             shape((n_pack, 16, GROUPS, 256), BF16),
             shape((n_pack, 8, 128), jnp.int32),
         ),
-        in_specs=[VM] * 6 + [ANY, VM, VM],
+        in_specs=[VM] * 4 + [ANY, VM, ANY, VM, VM],
         out_specs=(VM, VM),
         scratch_shapes=[
             pltpu.VMEM((16, ROWS, 128), BF16),
@@ -743,17 +753,18 @@
             pltpu.VMEM((D // 128, ROWS, 128), F32),
             pltpu.VMEM((16, 4, GROUPS, D), BF16),
             pltpu.VMEM((OUTC, 4 * D), BF16),
-            dma,
+            pltpu.VMEM((HEADS, HD, D), BF16),
+            dma((2,)),
             dma((16,)),
             dma((16,)),
             dma((64,)),
             dma((64,)),
             dma((n_pack,)),
             dma((n_pack,)),
-            dma((10 * nz,)),
-            dma((10 * nz,)),
-            dma((5 * nz,)),
-            dma((5 * nz,)),
+            dma((12 * nz,)),
+            dma((12 * nz,)),
+            dma((6 * nz,)),
+            dma((6 * nz,)),
         ],
         compiler_params=pltpu.CompilerParams(
             collective_id=1, has_side_effects=True, vmem_limit_bytes=60 * 2**20
@@ -775,7 +786,7 @@
         out_shape=shape((1, n_pack, MOST, OUTC), BF16),
         in_specs=[ANY, VM],
         out_specs=VM,
-        scratch_shapes=[pltpu.VMEM((n_pack, 4 * MOST, 256), BF16), dma((16,))],
+        scratch_shapes=[pltpu.VMEM((n_pack, 4 * MOST, 256), BF16), dma((32,))],
         compiler_params=pltpu.CompilerParams(vmem_limit_bytes=60 * 2**20),
         name="select",
     )(rows, tables)

time: 161 us -> 161 us (level)
  no operation moved by 1% of the time
where the time goes in v5:
time: 161 us; the launch traced here: 160 us
  Pallas kernels  160 us (99%)
    pallas_call x1, Pallas kernels, local(): pl.pallas_call(functools.partial(merge_kernel, n_pack), out_shape=(shape(...  97.3 us
    pallas_call x1, Pallas kernels, local(): pl.pallas_call(qkv_kernel, out_shape=(shape((4, 2, 3 * HD, 2 * ROWS), BF1...  42.4 us
    pallas_call x1, Pallas kernels, local(): pl.pallas_call(functools.partial(attention_kernel, n_pack), out_shape=(sh...  14.9 us
    pallas_call x1, Pallas kernels, local(): pl.pallas_call(functools.partial(select_kernel, n_pack), out_shape=shape(...  5.67 us

profile of v5, /device:TPU:1, one launch (start us, length us, event | category | flops | bytes accessed | tf_op | source)
XLA Modules:
  0.0 160.5 jit_solution(13994166781130203445)
XLA Ops:
  0.0 42.4 %qkv.1 = (bf16[4,2,264,384]{3,2,1,0:T(8,128)(2,1)}, s32[16,8,192]{2,1,0:T(8,128)}) custom-call(bf16[1,192,1408]{2,1,0:T(8,128)(2,1)} %patches_ref.3, s32[1,192]{1,0:T(1,128)} %mask_ref.3, bf16[1408]{0:T(1024)(128)(2,1)} %embed_ref.3, bf16[1408]{0:T(1024)(128)(2,1)} %gain_ref.2, bf16[264,1408]{1,0:T(8,128)(2,1)} %bitcast.5, s32[1,192]{1,0:T(1,128)} %seg_ref.1, ...), custom_call_target="tpu_custom_call" | custom-call | tf_op jit(solution)/shard_map/qkv/pallas_call | solution.py:691
  42.4 14.9 %attention.1 = (bf16[16,192,128]{2,1,0:T(8,128)(2,1)}, s32[8,128]{1,0:T(8,128)}) custom-call(bf16[4,2,264,384]{3,2,1,0:T(8,128)(2,1)} %get-tuple-element.11.qkv_ref, s32[16,8,192]{2,1,0:T(8,128)} %get-tuple-element.12.labels_ref, s32[1,8]{1,0:T(1,128)} %owner_ref.1), custom_call_target="tpu_custom_call" | custom-call | tf_op jit(solution)/shard_map/attention/pallas_call | solution.py:727
  57.3 97.3 %merge.1 = (bf16[16,16,48,256]{3,2,1,0:T(8,128)(2,1)}, s32[16,8,128]{2,1,0:T(8,128)}) custom-call(bf16[16,192,128]{2,1,0:T(8,128)(2,1)} %get-tuple-element.13.att_ref, bf16[1,192,1408]{2,1,0:T(8,128)(2,1)} %patches_ref.3, s32[1,192]{1,0:T(1,128)} %mask_ref.3, bf16[1408]{0:T(1024)(128)(2,1)} %embed_ref.3, bf16[16,88,1408]{2,1,0:T(8,128)(2,1)} %bitcast.3, ...), custom_call_target="tpu_custom_call" | custom-call | tf_op jit(solution)/shard_map/merge/pallas_call | solution.py:742
  154.6 5.7 %select.1 = bf16[1,16,192,224]{3,2,1,0:T(8,128)(2,1)} custom-call(bf16[16,16,48,256]{3,2,1,0:T(8,128)(2,1)} %get-tuple-element.15.arrived_ref, s32[16,8,128]{2,1,0:T(8,128)} %get-tuple-element.16.tables_ref), custom_call_target="tpu_custom_call" | custom-call | tf_op jit(solution)/shard_map/select/pallas_call | solution.py:784
